TPU v7x, 32 devices: a whole 2x2x4 slice. The times are simulated.
32 devices in a mesh: freq: 2 (over y), slab: 16 (over z, x, core).
Axes of the slice: x: 2, y: 2, z: 4, core: 2. Of those that a mesh axis runs over, the one named last changes fastest.
Arguments:
- wavefield: float32 [2, 2, 2048, 2048], P(None, 'freq', 'slab'), may hold values from -6 to 6
- freqs: float32 [2], P('freq'), may hold values from 0.15 to 0.45
- velocity: float32 [3, 2048, 2048], P(None, 'slab', 'freq'), may hold values from 0.7 to 1.6
- ref_slow: float32 [3, 2], replicated, may hold values from 0.6 to 1.5, as said below
Outputs:
- migrated: float32 [2, 2, 2048, 2048], P(None, 'freq', 'slab')
Inputs may be any that keep to these rules, and one draw needn't show every extreme that they name: ref_slow[d, 1] - ref_slow[d, 0] lies between 0.3 and 0.6 for every depth step.
All inputs are finite; a program needn't handle non-finite values.
Results may differ from a plain program's by a relative error of at most 0.0003.
Values sent between devices are 32-bit elements; how exact they have to be, the bound alone decides.
A program may use at most 64 MiB of HBM per device.

v0:
```python
import math

import jax
import jax.numpy as jnp
from jax import lax
from jax.sharding import PartitionSpec as P

two_pi = 2.0 * math.pi
depth_step = 2.0


def dft_matrix(length, sign):
    index = jnp.arange(length, dtype=jnp.int32)
    product = index[:, None] * index[None, :] % length
    angle = sign * two_pi / length * product.astype(jnp.float32)
    scale = 1.0 / math.sqrt(length)
    return (jnp.cos(angle) * scale, jnp.sin(angle) * scale)


def twiddle(outer, inner, sign):
    length = outer * inner
    product = (
        jnp.arange(outer, dtype=jnp.int32)[:, None]
        * jnp.arange(inner, dtype=jnp.int32)[None, :]
        % length
    )
    angle = sign * two_pi / length * product.astype(jnp.float32)
    return (jnp.cos(angle), jnp.sin(angle))


def complex_mix(form, mat_real, mat_imag, data_real, data_imag):

    def product(matrix, data):
        return jnp.einsum(form, matrix, data, precision=lax.Precision.HIGHEST)

    return (
        product(mat_real, data_real) - product(mat_imag, data_imag),
        product(mat_real, data_imag) + product(mat_imag, data_real),
    )


def transform(real, imag, trailing, sign):
    length = real.shape[-2] if trailing else real.shape[-1]
    inner = min(length, 128)
    outer = length // inner
    outer_real, outer_imag = dft_matrix(outer, sign)
    inner_real, inner_imag = dft_matrix(inner, sign)
    turn_real, turn_imag = twiddle(outer, inner, sign)
    if trailing:
        leading = real.shape[:-2]
        tail = real.shape[-1:]
        form_outer = "ka,...abm->...kbm"
        form_inner = "bj,...kbm->...kjm"
        turn_real = turn_real[:, :, None]
        turn_imag = turn_imag[:, :, None]
    else:
        leading = real.shape[:-1]
        tail = ()
        form_outer = "ka,...ab->...kb"
        form_inner = "bj,...kb->...kj"
    split_shape = leading + (outer, inner) + tail
    real = real.reshape(split_shape)
    imag = imag.reshape(split_shape)
    if sign < 0:
        real, imag = complex_mix(form_outer, outer_real, outer_imag, real, imag)
        real, imag = (real * turn_real - imag * turn_imag, real * turn_imag + imag * turn_real)
        real, imag = complex_mix(form_inner, inner_real, inner_imag, real, imag)
    else:
        real, imag = complex_mix(form_inner, inner_real, inner_imag, real, imag)
        real, imag = (real * turn_real - imag * turn_imag, real * turn_imag + imag * turn_real)
        real, imag = complex_mix(form_outer, outer_real, outer_imag, real, imag)
    joined = leading + (length,) + tail
    return (real.reshape(joined), imag.reshape(joined))


def wave_numbers(positions, length):
    inner = min(length, 128)
    outer = length // inner
    number = positions // inner + outer * (positions % inner)
    number = jnp.where(number < length // 2, number, number - length)
    return number.astype(jnp.float32) / length


def forward_x(items):
    real, imag = transform(items[0], items[1], True, -1)
    return jnp.stack((real, imag))


def inverse_y(items):
    real, imag = transform(items[:, 0], items[:, 1], False, 1)
    return jnp.stack((real, imag), axis=1)


def shards(wavefield, freqs, velocity, ref_slow):
    slabs = lax.axis_size("slab")
    slab_index = lax.axis_index("slab")
    rows = wavefield.shape[2]
    width_x = rows * slabs
    width_y = wavefield.shape[3]
    columns = width_y // slabs
    depth = ref_slow.shape[0]
    along_x = wave_numbers(jnp.arange(width_x, dtype=jnp.int32), width_x)
    along_y = wave_numbers(slab_index * columns + jnp.arange(columns, dtype=jnp.int32), width_y)
    square = along_x[:, None] ** 2 + along_y[None, :] ** 2
    freq_col = freqs[:, None, None]

    def advance(level, field):
        local_tile = lax.dynamic_index_in_dim(velocity, level, 0, keepdims=False)
        tile = lax.all_gather(local_tile, "freq", axis=1, tiled=True)
        real, imag = transform(field[0], field[1], False, -1)
        spectrum = forward_x(
            lax.all_to_all(jnp.stack((real, imag)), "slab", split_axis=3, concat_axis=2, tiled=True)
        )
        slow_pair = lax.dynamic_index_in_dim(ref_slow, level, 0, keepdims=False)
        slowness = 1.0 / tile
        upper_weight = jnp.clip((slowness - slow_pair[0]) / (slow_pair[1] - slow_pair[0]), 0.0, 1.0)
        weights = [1.0 - upper_weight, upper_weight]
        shifted = []
        for branch in range(2):
            target = (freq_col * slow_pair[branch]) ** 2 - square[None]
            angle = two_pi * depth_step * jnp.sqrt(jnp.abs(target))
            live = target >= 0
            prop_real = jnp.where(live, jnp.cos(angle), jnp.exp(-angle))
            prop_imag = jnp.where(live, jnp.sin(angle), jnp.zeros_like(angle))
            spec_real = spectrum[0] * prop_real - spectrum[1] * prop_imag
            spec_imag = spectrum[0] * prop_imag + spectrum[1] * prop_real
            back_real, back_imag = transform(spec_real, spec_imag, True, 1)
            shifted.append(jnp.stack((back_real, back_imag)))
        pieces = []
        for branch in range(2):
            moved = lax.all_to_all(shifted[branch], "slab", split_axis=2, concat_axis=3, tiled=True)
            pieces.append(inverse_y(moved[None])[0])
        spatial = jnp.stack(pieces)
        new_real = jnp.zeros_like(field[0])
        new_imag = jnp.zeros_like(field[1])
        for branch in range(2):
            theta = two_pi * depth_step * freq_col * (slowness - slow_pair[branch])[None]
            weight = weights[branch][None]
            cosine = jnp.cos(theta)
            sine = jnp.sin(theta)
            part_real = spatial[branch, 0]
            part_imag = spatial[branch, 1]
            new_real = new_real + weight * (cosine * part_real - sine * part_imag)
            new_imag = new_imag + weight * (cosine * part_imag + sine * part_real)
        return jnp.stack((new_real, new_imag))

    return lax.fori_loop(0, depth, advance, wavefield)


def solution(mesh):
    return jax.shard_map(
        shards,
        mesh=mesh,
        in_specs=(P(None, "freq", "slab", None), P("freq"), P(None, "slab", "freq"), P()),
        out_specs=P(None, "freq", "slab", None),
        check_vma=False,
    )
```

profile of v0, /device:TPU:11, one launch (start us, length us, event | category | flops | bytes accessed | tf_op | source)
XLA Modules:
  0.0 790.6 jit_solution(8718204456309350147)
XLA Ops:
  8.1 774.4 %while.17 = (s32[]{:T(128)}, f32[2,1,128,2048]{3,2,1,0:T(8,128)S(1)}, f32[3,128,1024]{2,1,0:T(8,128)}, f32[3,2]{0,1:T(2,128)S(1)}, f32[1,1,1]{2,1,0:T(1,128)}, /...) while((s32[]{:T(128)}, f32[2,1,128,2048]{3,2,1,0:T(8,128)S(1)}, ...), condition=%wide.region_1.2_spmd.clone, body=%wide.region_0.1_spmd.clone.sunk | while | flops 10909407232 | bytes 317449280 | solution.py:147
  23.0 6.5 all-to-all-start
  32.9 10.2 %fusion.669 = (f32[2048,128]{1,0:T(8,128)}, f32[2048,128]{1,0:T(8,128)}, f32[2048,128]{1,0:T(8,128)S(1)}, f32[2048,128]{1,0:T(8,128)}) fusion(f32[128]{0:T(128)S(1)} %get-tuple-element.413, f32[2048]{0:T(1024)S(1)} %get-tuple-element.414, f32[]{:T(128)} %bitcast.650, f32[]{:T(128)} %bitcast.652), kind=kLoop, calls=%fused_computation.62.clone.1 | loop fusion | flops 3932160 | bytes 4203016 | tf_op jit(solution)/shard_map/while/body/eval_jaxpr/jit(_where)/select_n | solution.py:124
  52.1 24.8 %all-to-all-done = f32[2,1,128,2048]{2,1,0,3:T(1,128)S(1)} async-done(((f32[2,1,128,2048]{2,1,0,3:T(1,128)}), f32[2,1,128,2048]{2,1,0,3:T(1,128)S(1)}, u32[]{:S(2)}, u32[]{:S(2)}) %all-to-all-start) | async-done | bytes 2097184 | tf_op jit(solution)/shard_map/while/body/eval_jaxpr/all_to_all | solution.py:112
  114.7 10.2 %copy.403 = f32[2,1,2048,128]{3,1,0,2:T(1,128)} copy(f32[2,1,2048,128]{3,2,1,0:T(8,128)S(1)} %pad_maximum_fusion.10) | data formatting | bytes 4194304 | tf_op jit(solution)/shard_map/while/body/eval_jaxpr/stack | solution.py:128
  136.0 10.0 %copy.396 = f32[2,1,2048,128]{3,1,0,2:T(1,128)} copy(f32[2,1,2048,128]{3,2,1,0:T(8,128)S(1)} %pad_maximum_fusion.9) | data formatting | bytes 4194304 | tf_op jit(solution)/shard_map/while/body/eval_jaxpr/stack | solution.py:128
  145.9 31.4 %all-to-all-done.2 = f32[2,1,2048,128]{3,1,0,2:T(1,128)} async-done(((f32[2,1,2048,128]{3,1,0,2:T(1,128)}), f32[2,1,2048,128]{3,1,0,2:T(1,128)}, u32[]{:S(2)}, u32[]{:S(2)}) %all-to-all-start.2) | async-done | bytes 2097184 | tf_op jit(solution)/shard_map/while/body/eval_jaxpr/all_to_all | solution.py:131
  202.3 27.2 %all-to-all-done.1 = f32[2,1,2048,128]{3,1,0,2:T(1,128)S(1)} async-done(((f32[2,1,2048,128]{3,1,0,2:T(1,128)}), f32[2,1,2048,128]{3,1,0,2:T(1,128)S(1)}, u32[]{:S(2)}, u32[]{:S(2)}) %all-to-all-start.1) | async-done | bytes 2097184 | tf_op jit(solution)/shard_map/while/body/eval_jaxpr/all_to_all | solution.py:131
  255.7 10.9 %fusion.706 = (f32[1,1,128,2048]{3,2,1,0:T(8,128)S(1)}, f32[1,1,128,2048]{3,2,1,0:T(8,128)S(1)}) fusion(f32[16,8,16,128]{3,2,1,0:T(8,128)} %bitcast.711, f32[16,8,16,128]{3,2,1,0:T(8,128)S(1)} %bitcast.710, f32[16,8,16,128]{3,2,1,0:T(8,128)S(1)} %bitcast.709, f32[16,8,16,128]{3,2,1,0:T(8,128)S(1)} %bitcast.708, f32[]{:T(128)} %bitcast.679, ...), kind=kLoop, calls=%fused_computation.70.clone.1 | loop fusion | flops 6815744 | bytes 7340048 | tf_op jit(solution)/shard_map/while/body/eval_jaxpr/stack | solution.py:145
  290.1 10.2 %fusion.669 = (f32[2048,128]{1,0:T(8,128)}, f32[2048,128]{1,0:T(8,128)}, f32[2048,128]{1,0:T(8,128)S(1)}, f32[2048,128]{1,0:T(8,128)}) fusion(f32[128]{0:T(128)S(1)} %get-tuple-element.413, f32[2048]{0:T(1024)S(1)} %get-tuple-element.414, f32[]{:T(128)} %bitcast.650, f32[]{:T(128)} %bitcast.652), kind=kLoop, calls=%fused_computation.62.clone.1 | loop fusion | flops 3932160 | bytes 4203016 | tf_op jit(solution)/shard_map/while/body/eval_jaxpr/jit(_where)/select_n | solution.py:124
  309.3 24.8 %all-to-all-done = f32[2,1,128,2048]{2,1,0,3:T(1,128)S(1)} async-done(((f32[2,1,128,2048]{2,1,0,3:T(1,128)}), f32[2,1,128,2048]{2,1,0,3:T(1,128)S(1)}, u32[]{:S(2)}, u32[]{:S(2)}) %all-to-all-start) | async-done | bytes 2097184 | tf_op jit(solution)/shard_map/while/body/eval_jaxpr/all_to_all | solution.py:112
  371.8 10.2 %copy.403 = f32[2,1,2048,128]{3,1,0,2:T(1,128)} copy(f32[2,1,2048,128]{3,2,1,0:T(8,128)S(1)} %pad_maximum_fusion.10) | data formatting | bytes 4194304 | tf_op jit(solution)/shard_map/while/body/eval_jaxpr/stack | solution.py:128
  393.0 10.0 %copy.396 = f32[2,1,2048,128]{3,1,0,2:T(1,128)} copy(f32[2,1,2048,128]{3,2,1,0:T(8,128)S(1)} %pad_maximum_fusion.9) | data formatting | bytes 4194304 | tf_op jit(solution)/shard_map/while/body/eval_jaxpr/stack | solution.py:128
  403.0 31.4 %all-to-all-done.2 = f32[2,1,2048,128]{3,1,0,2:T(1,128)} async-done(((f32[2,1,2048,128]{3,1,0,2:T(1,128)}), f32[2,1,2048,128]{3,1,0,2:T(1,128)}, u32[]{:S(2)}, u32[]{:S(2)}) %all-to-all-start.2) | async-done | bytes 2097184 | tf_op jit(solution)/shard_map/while/body/eval_jaxpr/all_to_all | solution.py:131
  459.2 27.4 %all-to-all-done.1 = f32[2,1,2048,128]{3,1,0,2:T(1,128)S(1)} async-done(((f32[2,1,2048,128]{3,1,0,2:T(1,128)}), f32[2,1,2048,128]{3,1,0,2:T(1,128)S(1)}, u32[]{:S(2)}, u32[]{:S(2)}) %all-to-all-start.1) | async-done | bytes 2097184 | tf_op jit(solution)/shard_map/while/body/eval_jaxpr/all_to_all | solution.py:131
  513.0 10.9 %fusion.706 = (f32[1,1,128,2048]{3,2,1,0:T(8,128)S(1)}, f32[1,1,128,2048]{3,2,1,0:T(8,128)S(1)}) fusion(f32[16,8,16,128]{3,2,1,0:T(8,128)} %bitcast.711, f32[16,8,16,128]{3,2,1,0:T(8,128)S(1)} %bitcast.710, f32[16,8,16,128]{3,2,1,0:T(8,128)S(1)} %bitcast.709, f32[16,8,16,128]{3,2,1,0:T(8,128)S(1)} %bitcast.708, f32[]{:T(128)} %bitcast.679, ...), kind=kLoop, calls=%fused_computation.70.clone.1 | loop fusion | flops 6815744 | bytes 7340048 | tf_op jit(solution)/shard_map/while/body/eval_jaxpr/stack | solution.py:145
  547.4 10.2 %fusion.669 = (f32[2048,128]{1,0:T(8,128)}, f32[2048,128]{1,0:T(8,128)}, f32[2048,128]{1,0:T(8,128)S(1)}, f32[2048,128]{1,0:T(8,128)}) fusion(f32[128]{0:T(128)S(1)} %get-tuple-element.413, f32[2048]{0:T(1024)S(1)} %get-tuple-element.414, f32[]{:T(128)} %bitcast.650, f32[]{:T(128)} %bitcast.652), kind=kLoop, calls=%fused_computation.62.clone.1 | loop fusion | flops 3932160 | bytes 4203016 | tf_op jit(solution)/shard_map/while/body/eval_jaxpr/jit(_where)/select_n | solution.py:124
  566.6 24.8 %all-to-all-done = f32[2,1,128,2048]{2,1,0,3:T(1,128)S(1)} async-done(((f32[2,1,128,2048]{2,1,0,3:T(1,128)}), f32[2,1,128,2048]{2,1,0,3:T(1,128)S(1)}, u32[]{:S(2)}, u32[]{:S(2)}) %all-to-all-start) | async-done | bytes 2097184 | tf_op jit(solution)/shard_map/while/body/eval_jaxpr/all_to_all | solution.py:112
  628.9 10.4 %copy.403 = f32[2,1,2048,128]{3,1,0,2:T(1,128)} copy(f32[2,1,2048,128]{3,2,1,0:T(8,128)S(1)} %pad_maximum_fusion.10) | data formatting | bytes 4194304 | tf_op jit(solution)/shard_map/while/body/eval_jaxpr/stack | solution.py:128
  639.3 4.9 all-to-all-start.2
  650.3 10.0 %copy.396 = f32[2,1,2048,128]{3,1,0,2:T(1,128)} copy(f32[2,1,2048,128]{3,2,1,0:T(8,128)S(1)} %pad_maximum_fusion.9) | data formatting | bytes 4194304 | tf_op jit(solution)/shard_map/while/body/eval_jaxpr/stack | solution.py:128
  660.3 31.4 %all-to-all-done.2 = f32[2,1,2048,128]{3,1,0,2:T(1,128)} async-done(((f32[2,1,2048,128]{3,1,0,2:T(1,128)}), f32[2,1,2048,128]{3,1,0,2:T(1,128)}, u32[]{:S(2)}, u32[]{:S(2)}) %all-to-all-start.2) | async-done | bytes 2097184 | tf_op jit(solution)/shard_map/while/body/eval_jaxpr/all_to_all | solution.py:131
  716.4 27.5 %all-to-all-done.1 = f32[2,1,2048,128]{3,1,0,2:T(1,128)S(1)} async-done(((f32[2,1,2048,128]{3,1,0,2:T(1,128)}), f32[2,1,2048,128]{3,1,0,2:T(1,128)S(1)}, u32[]{:S(2)}, u32[]{:S(2)}) %all-to-all-start.1) | async-done | bytes 2097184 | tf_op jit(solution)/shard_map/while/body/eval_jaxpr/all_to_all | solution.py:131
  770.3 10.9 %fusion.706 = (f32[1,1,128,2048]{3,2,1,0:T(8,128)S(1)}, f32[1,1,128,2048]{3,2,1,0:T(8,128)S(1)}) fusion(f32[16,8,16,128]{3,2,1,0:T(8,128)} %bitcast.711, f32[16,8,16,128]{3,2,1,0:T(8,128)S(1)} %bitcast.710, f32[16,8,16,128]{3,2,1,0:T(8,128)S(1)} %bitcast.709, f32[16,8,16,128]{3,2,1,0:T(8,128)S(1)} %bitcast.708, f32[]{:T(128)} %bitcast.679, ...), kind=kLoop, calls=%fused_computation.70.clone.1 | loop fusion | flops 6815744 | bytes 7340048 | tf_op jit(solution)/shard_map/while/body/eval_jaxpr/stack | solution.py:145
  (324 shorter events, 375.6 us)
Async XLA Ops:
  23.0 53.9 %all-to-all-start = ((f32[2,1,128,2048]{2,1,0,3:T(1,128)}), f32[2,1,128,2048]{2,1,0,3:T(1,128)S(1)}, u32[]{:S(2)}, u32[]{:S(2)}) async-start(f32[2,1,128,2048]{2,1,0,3:T(1,128)} %pad_maximum_fusion.8), calls=%async_computation | async-start | bytes 4194304 | tf_op jit(solution)/shard_map/while/body/eval_jaxpr/all_to_all | solution.py:112
  89.8 2.5 copy-start.7
  91.1 1.8 copy-start.6
  124.9 4.9 copy-start.2
  124.9 52.4 %all-to-all-start.2 = ((f32[2,1,2048,128]{3,1,0,2:T(1,128)}), f32[2,1,2048,128]{3,1,0,2:T(1,128)}, u32[]{:S(2)}, u32[]{:S(2)}) async-start(f32[2,1,2048,128]{3,1,0,2:T(1,128)} %copy.403), calls=%async_computation.2 | async-start | bytes 4194304 | tf_op jit(solution)/shard_map/while/body/eval_jaxpr/all_to_all | solution.py:131
  177.3 52.2 %all-to-all-start.1 = ((f32[2,1,2048,128]{3,1,0,2:T(1,128)}), f32[2,1,2048,128]{3,1,0,2:T(1,128)S(1)}, u32[]{:S(2)}, u32[]{:S(2)}) async-start(f32[2,1,2048,128]{3,1,0,2:T(1,128)} %copy.396), calls=%async_computation.1 | async-start | bytes 4194304 | tf_op jit(solution)/shard_map/while/body/eval_jaxpr/all_to_all | solution.py:131
  182.1 73.6 %all-gather.6.cloned.1.call-start = ((), (), s32[]{:S(2)}) async-start(), calls=%async_computation.3 | async-start | bytes 1572864 | tf_op jit(solution)/shard_map/while/body/eval_jaxpr/all_gather | solution.py:109
  235.2 3.9 copy-start.1
  282.0 52.2 %all-to-all-start = ((f32[2,1,128,2048]{2,1,0,3:T(1,128)}), f32[2,1,128,2048]{2,1,0,3:T(1,128)S(1)}, u32[]{:S(2)}, u32[]{:S(2)}) async-start(f32[2,1,128,2048]{2,1,0,3:T(1,128)} %pad_maximum_fusion.8), calls=%async_computation | async-start | bytes 4194304 | tf_op jit(solution)/shard_map/while/body/eval_jaxpr/all_to_all | solution.py:112
  346.7 2.5 copy-start.7
  348.0 1.8 copy-start.6
  382.0 4.9 copy-start.2
  382.0 52.4 %all-to-all-start.2 = ((f32[2,1,2048,128]{3,1,0,2:T(1,128)}), f32[2,1,2048,128]{3,1,0,2:T(1,128)}, u32[]{:S(2)}, u32[]{:S(2)}) async-start(f32[2,1,2048,128]{3,1,0,2:T(1,128)} %copy.403), calls=%async_computation.2 | async-start | bytes 4194304 | tf_op jit(solution)/shard_map/while/body/eval_jaxpr/all_to_all | solution.py:131
  434.4 52.2 %all-to-all-start.1 = ((f32[2,1,2048,128]{3,1,0,2:T(1,128)}), f32[2,1,2048,128]{3,1,0,2:T(1,128)S(1)}, u32[]{:S(2)}, u32[]{:S(2)}) async-start(f32[2,1,2048,128]{3,1,0,2:T(1,128)} %copy.396), calls=%async_computation.1 | async-start | bytes 4194304 | tf_op jit(solution)/shard_map/while/body/eval_jaxpr/all_to_all | solution.py:131
  439.2 73.8 %all-gather.6.cloned.1.call-start = ((), (), s32[]{:S(2)}) async-start(), calls=%async_computation.3 | async-start | bytes 1572864 | tf_op jit(solution)/shard_map/while/body/eval_jaxpr/all_gather | solution.py:109
  492.5 3.9 copy-start.1
  539.3 52.2 %all-to-all-start = ((f32[2,1,128,2048]{2,1,0,3:T(1,128)}), f32[2,1,128,2048]{2,1,0,3:T(1,128)S(1)}, u32[]{:S(2)}, u32[]{:S(2)}) async-start(f32[2,1,128,2048]{2,1,0,3:T(1,128)} %pad_maximum_fusion.8), calls=%async_computation | async-start | bytes 4194304 | tf_op jit(solution)/shard_map/while/body/eval_jaxpr/all_to_all | solution.py:112
  603.9 2.5 copy-start.7
  605.2 1.8 copy-start.6
  639.3 4.9 copy-start.2
  639.3 52.4 %all-to-all-start.2 = ((f32[2,1,2048,128]{3,1,0,2:T(1,128)}), f32[2,1,2048,128]{3,1,0,2:T(1,128)}, u32[]{:S(2)}, u32[]{:S(2)}) async-start(f32[2,1,2048,128]{3,1,0,2:T(1,128)} %copy.403), calls=%async_computation.2 | async-start | bytes 4194304 | tf_op jit(solution)/shard_map/while/body/eval_jaxpr/all_to_all | solution.py:131
  691.7 52.2 %all-to-all-start.1 = ((f32[2,1,2048,128]{3,1,0,2:T(1,128)}), f32[2,1,2048,128]{3,1,0,2:T(1,128)S(1)}, u32[]{:S(2)}, u32[]{:S(2)}) async-start(f32[2,1,2048,128]{3,1,0,2:T(1,128)} %copy.396), calls=%async_computation.1 | async-start | bytes 4194304 | tf_op jit(solution)/shard_map/while/body/eval_jaxpr/all_to_all | solution.py:131
  696.5 73.8 %all-gather.6.cloned.1.call-start = ((), (), s32[]{:S(2)}) async-start(), calls=%async_computation.3 | async-start | bytes 1572864 | tf_op jit(solution)/shard_map/while/body/eval_jaxpr/all_gather | solution.py:109
  749.6 3.9 copy-start.1
  (15 other events, 20.7 us)
Sparse Core Ops, SparseCore 0:
  184.5 21.7 all-gather.5
  441.5 21.7 all-gather.5
  698.8 21.7 all-gather.5
where the time goes:
time: 794 us; the launch traced here: 791 us
  waiting for transfers between devices  251 us (32%)
  matrix products  223 us (28%)
  local copies, waits for them, and re-layouts  167 us (21%)
  other arithmetic  75.2 us (9%)
  starting transfers between devices  45.2 us (6%)
  loops' own time  14.6 us (2%)
  between operations  14.1 us (2%)
    dot_general x144, matrix products, product(): return jnp.einsum(form, matrix, data, precision=lax.Precision.HIGHEST)  223 us
    all_to_all x6, waiting for transfers between devices, advance(): lax.all_to_all(shifted[branch], 'slab', split_axis=2, concat_axis=3, tile...  176 us
    all_to_all x3, waiting for transfers between devices, advance(): lax.all_to_all(jnp.stack((real, imag)), 'slab', split_axis=3, concat_axis...  74.5 us
    another operation x6, local copies, waits for them, and re-layouts, advance(): shifted.append(jnp.stack((back_real, back_imag)))  60.7 us
    another operation x6, other arithmetic, advance(): return jnp.stack((new_real, new_imag))  33.4 us
    select_n x3, other arithmetic, advance(): prop_imag = jnp.where(live, jnp.sin(angle), jnp.zeros_like(angle))  30.7 us
    all_to_all x12, local copies, waits for them, and re-layouts, advance(): lax.all_to_all(shifted[branch], 'slab', split_axis=2, concat_axis=3, tile...  29.5 us
    all_to_all x6, starting transfers between devices, advance(): lax.all_to_all(shifted[branch], 'slab', split_axis=2, concat_axis=3, tile...  29 us
  transfers between devices with their start and end apart: 12, of which 9 were waited for; matrix products, arithmetic and copies ran while one was open for 31% of the time, Pallas kernels for 0%

commit v1 on v0

--- a/solution.py
+++ b/solution.py
@@ -1,8 +1,12 @@
+import functools
 import math
 
 import jax
 import jax.numpy as jnp
+import numpy as np
 from jax import lax
+from jax.experimental import pallas as pl
+from jax.experimental.pallas import tpu as pltpu
 from jax.sharding import PartitionSpec as P
 
 two_pi = 2.0 * math.pi
@@ -91,7 +95,7 @@
     return jnp.stack((real, imag), axis=1)
 
 
-def shards(wavefield, freqs, velocity, ref_slow):
+def shards_generic(wavefield, freqs, velocity, ref_slow):
     slabs = lax.axis_size("slab")
     slab_index = lax.axis_index("slab")
     rows = wavefield.shape[2]
@@ -147,11 +151,385 @@
     return lax.fori_loop(0, depth, advance, wavefield)
 
 
+LANES = 128
+ROWS = 8
+VMEM_LIMIT = 56 * 2**20
+
+
+def turn(numerator, denominator, sign):
+    angle = sign * 2.0 * np.pi * ((numerator % denominator) / denominator)
+    return (np.cos(angle), np.sin(angle))
+
+
+def times(real, imag, c, s):
+    if abs(s) < 1e-12:
+        return (real, imag) if c > 0 else (-real, -imag)
+    if abs(c) < 1e-12:
+        return (-imag, real) if s > 0 else (imag, -real)
+    if abs(abs(c) - abs(s)) < 1e-12:
+        k = float(abs(c))
+        a, b = (k if c > 0 else -k), (s > 0) == (c > 0)
+        if b:
+            return ((real - imag) * a, (real + imag) * a)
+        return ((real + imag) * a, (imag - real) * a)
+    c, s = float(c), float(s)
+    return (real * c - imag * s, real * s + imag * c)
+
+
+def small_fft(real, imag, sign):
+    count = len(real)
+    if count == 1:
+        return real, imag
+    er, ei = small_fft(real[0::2], imag[0::2], sign)
+    odd_r, odd_i = small_fft(real[1::2], imag[1::2], sign)
+    low, high = [], []
+    for k in range(count // 2):
+        tr, ti = times(odd_r[k], odd_i[k], *turn(k, count, sign))
+        low.append((er[k] + tr, ei[k] + ti))
+        high.append((er[k] - tr, ei[k] - ti))
+    both = low + high
+    return [v[0] for v in both], [v[1] for v in both]
+
+
+def halves(x):
+    high = x.astype(jnp.bfloat16)
+    low = (x - high.astype(jnp.float32)).astype(jnp.bfloat16)
+    return high, low
+
+
+def product(a, b):
+    def dot(p, q):
+        return jnp.dot(p, q, preferred_element_type=jnp.float32)
+
+    return dot(a[0], b[0]) + (dot(a[0], b[1]) + dot(a[1], b[0]))
+
+
+def matrix_of(inner, length, sign, left):
+    index = np.arange(inner)
+    angle = sign * 2.0 * np.pi * ((index[:, None] * index[None, :]) % inner) / inner
+    c = np.cos(angle) / np.sqrt(length)
+    s = np.sin(angle) / np.sqrt(length)
+    full = np.block([[c, -s], [s, c]]) if left else np.block([[c, s], [-s, c]])
+    full = full.astype(np.float32)
+    high = full.astype(jnp.bfloat16)
+    low = (full - high.astype(np.float32)).astype(jnp.bfloat16)
+    return np.stack([high, low])
+
+
+def twiddle_table(outer, inner, rows):
+    c, s = turn(np.arange(outer)[:, None] * np.arange(inner)[None, :], outer * inner, -1)
+    both = np.stack([c, s], axis=1).astype(np.float32)
+    if rows:
+        return np.ascontiguousarray(np.broadcast_to(both[:, :, :, None], (outer, 2, inner, LANES)))
+    return np.ascontiguousarray(np.broadcast_to(both[:, :, None, :], (outer, 2, ROWS, inner)))
+
+
+def cosine_terms():
+    z = 0.125 + 0.125 * np.cos(np.pi * (np.arange(400) + 0.5) / 400)
+    r = np.sqrt(z)
+
+    def fit(values, degree):
+        poly = np.polynomial.Chebyshev.fit(z, values, degree, domain=[0.0, 0.25])
+        poly = poly.convert(kind=np.polynomial.Polynomial)
+        return [float(np.float32(v)) for v in poly.coef]
+
+    return fit(np.cos(2 * np.pi * r), 8), fit(np.sin(2 * np.pi * r) / r, 7)
+
+
+COS_TERMS, SIN_TERMS = cosine_terms()
+
+
+def horner(terms, z):
+    value = z * terms[-1] + terms[-2]
+    for term in terms[-3::-1]:
+        value = value * z + term
+    return value
+
+
+def circle(turns):
+    rest = turns - jnp.round(turns)
+    z = rest * rest
+    return horner(COS_TERMS, z), rest * horner(SIN_TERMS, z)
+
+
+def spread_kernel(outer, length, scal, fy2, out):
+    freq = scal[0]
+    rows = out.shape[3]
+
+    @pl.loop(0, outer)
+    def _(k1):
+        @pl.loop(0, rows // 32)
+        def _(c):
+            base = pl.multiple_of(c * 32, 32)
+            number = k1 + outer * (base + lax.broadcasted_iota(jnp.int32, (32, LANES), 0))
+            number = jnp.where(number < length // 2, number, number - length)
+            fx = number.astype(jnp.float32) * (1.0 / length)
+            square = fx * fx + fy2[0:1, :]
+            for branch in range(2):
+                wave = freq * scal[1 + branch]
+                target = wave * wave - square
+                turns = depth_step * jnp.sqrt(jnp.abs(target))
+                live = target >= 0
+                cosine, sine = circle(turns)
+                decay = jnp.exp(turns * (-two_pi))
+                out[branch, k1, 0, pl.ds(base, 32), :] = jnp.where(live, cosine, decay)
+                out[branch, k1, 1, pl.ds(base, 32), :] = jnp.where(live, sine, 0.0)
+
+
+def weight_kernel(scal, velocity, out):
+    freq = scal[0]
+    rows, width = velocity.shape
+
+    @pl.loop(0, rows // ROWS)
+    def _(c):
+        at = pl.ds(pl.multiple_of(c * ROWS, ROWS), ROWS)
+        for j in range(width // 512):
+            cols = slice(j * 512, (j + 1) * 512)
+            slowness = 1.0 / velocity[at, cols]
+            upper = jnp.clip((slowness - scal[1]) / (scal[2] - scal[1]), 0.0, 1.0)
+            for branch, weight in enumerate((1.0 - upper, upper)):
+                cosine, sine = circle(depth_step * freq * (slowness - scal[1 + branch]))
+                out[branch, 0, at, cols] = weight * cosine
+                out[branch, 1, at, cols] = weight * sine
+
+
+def row_out(mat, work, out):
+    outer, rows, double = work.shape
+    inner = double // 2
+
+    @pl.loop(0, outer // 2)
+    def _(g):
+        x = work[pl.ds(g * 2, 2)].reshape(2 * rows, double)
+        y = product(halves(x), (mat[0], mat[1])).reshape(2, rows, double)
+        for j in range(2):
+            out[g * 2 + j, 0] = y[j, :, :inner]
+            out[g * 2 + j, 1] = y[j, :, inner:]
+
+
+def twiddled(real, imag, tw, k):
+    c, s = tw[k, 0], tw[k, 1]
+    return real * c - imag * s, real * s + imag * c
+
+
+def conj_twiddled(real, imag, c, s):
+    return real * c + imag * s, imag * c - real * s
+
+
+def first_kernel(field, mat, tw, out, work):
+    outer, rows, double = work.shape
+    inner = double // 2
+
+    @pl.loop(0, rows // ROWS)
+    def _(c):
+        at = pl.ds(pl.multiple_of(c * ROWS, ROWS), ROWS)
+        real = [field[0, at, a * inner : (a + 1) * inner] for a in range(outer)]
+        imag = [field[1, at, a * inner : (a + 1) * inner] for a in range(outer)]
+        real, imag = small_fft(real, imag, -1)
+        for k in range(outer):
+            work[k, at, :inner], work[k, at, inner:] = twiddled(real[k], imag[k], tw, k)
+
+    row_out(mat, work, out)
+
+
+def column_forward_kernel(got, mat, tw, out, work):
+    outer, _, rows, lanes = got.shape
+
+    @pl.loop(0, rows // ROWS)
+    def _(c):
+        base = pl.multiple_of(c * ROWS, ROWS)
+        at = pl.ds(base, ROWS)
+        real = [got[a, 0, at, :] for a in range(outer)]
+        imag = [got[a, 1, at, :] for a in range(outer)]
+        real, imag = small_fft(real, imag, -1)
+        for k in range(outer):
+            cos, sin = tw[k, 0, at, :], tw[k, 1, at, :]
+            work[k, 0, at, :] = real[k] * cos - imag[k] * sin
+            work[k, 1, at, :] = real[k] * sin + imag[k] * cos
+
+    @pl.loop(0, outer // 2)
+    def _(g):
+        x = [work[g * 2 + j].reshape(2 * rows, lanes) for j in range(2)]
+        y = product((mat[0], mat[1]), halves(jnp.concatenate(x, axis=1)))
+        for j in range(2):
+            out[g * 2 + j] = y[:, j * lanes : (j + 1) * lanes].reshape(2, rows, lanes)
+
+
+def column_back_kernel(spec, shift, mat, tw, out, work):
+    outer, _, rows, lanes = spec.shape
+
+    @pl.loop(0, outer // 2)
+    def _(g):
+        parts = []
+        for j in range(2):
+            k = g * 2 + j
+            sr, si = spec[k, 0], spec[k, 1]
+            er, ei = shift[k, 0], shift[k, 1]
+            parts.append(jnp.concatenate([sr * er - si * ei, sr * ei + si * er], axis=0))
+        y = product((mat[0], mat[1]), halves(jnp.concatenate(parts, axis=1)))
+        for j in range(2):
+            k = g * 2 + j
+            z = y[:, j * lanes : (j + 1) * lanes]
+            work[k, 0], work[k, 1] = conj_twiddled(z[:rows], z[rows:], tw[k, 0], tw[k, 1])
+
+    @pl.loop(0, rows // ROWS)
+    def _(c):
+        at = pl.ds(pl.multiple_of(c * ROWS, ROWS), ROWS)
+        real = [work[k, 0, at, :] for k in range(outer)]
+        imag = [work[k, 1, at, :] for k in range(outer)]
+        real, imag = small_fft(real, imag, 1)
+        for a in range(outer):
+            out[a, 0, at, :] = real[a]
+            out[a, 1, at, :] = imag[a]
+
+
+def row_back(got, mat, tw, work):
+    outer, rows, double = work.shape
+    inner = double // 2
+
+    @pl.loop(0, outer // 2)
+    def _(g):
+        x = [jnp.concatenate([got[g * 2 + j, 0], got[g * 2 + j, 1]], axis=1) for j in range(2)]
+        y = product(halves(jnp.concatenate(x, axis=0)), (mat[0], mat[1])).reshape(2, rows // ROWS, ROWS, double)
+        for j in range(2):
+            k = g * 2 + j
+            c, s = tw[k, 0][None], tw[k, 1][None]
+            real, imag = conj_twiddled(y[j, :, :, :inner], y[j, :, :, inner:], c, s)
+            work[k, :, :inner] = real.reshape(rows, inner)
+            work[k, :, inner:] = imag.reshape(rows, inner)
+
+
+def row_back_kernel(got, weight, mat, tw, out, work):
+    outer, rows, double = work.shape
+    inner = double // 2
+    row_back(got, mat, tw, work)
+
+    @pl.loop(0, rows // ROWS)
+    def _(c):
+        at = pl.ds(pl.multiple_of(c * ROWS, ROWS), ROWS)
+        real = [work[k, at, :inner] for k in range(outer)]
+        imag = [work[k, at, inner:] for k in range(outer)]
+        real, imag = small_fft(real, imag, 1)
+        for a in range(outer):
+            cols = slice(a * inner, (a + 1) * inner)
+            wr, wi = weight[0, at, cols], weight[1, at, cols]
+            out[0, at, cols] = real[a] * wr - imag[a] * wi
+            out[1, at, cols] = real[a] * wi + imag[a] * wr
+
+
+def row_join_kernel(last, got, weight, part, mat, tw, mat_next, out, work):
+    outer, rows, double = work.shape
+    inner = double // 2
+    row_back(got, mat, tw, work)
+
+    @pl.loop(0, rows // ROWS)
+    def _(c):
+        at = pl.ds(pl.multiple_of(c * ROWS, ROWS), ROWS)
+        real = [work[k, at, :inner] for k in range(outer)]
+        imag = [work[k, at, inner:] for k in range(outer)]
+        real, imag = small_fft(real, imag, 1)
+        new_real, new_imag = [], []
+        for a in range(outer):
+            cols = slice(a * inner, (a + 1) * inner)
+            wr, wi = weight[0, at, cols], weight[1, at, cols]
+            new_real.append(part[0, at, cols] + (real[a] * wr - imag[a] * wi))
+            new_imag.append(part[1, at, cols] + (real[a] * wi + imag[a] * wr))
+        if last:
+            for a in range(outer):
+                cols = slice(a * inner, (a + 1) * inner)
+                out[0, at, cols] = new_real[a]
+                out[1, at, cols] = new_imag[a]
+        else:
+            real, imag = small_fft(new_real, new_imag, -1)
+            for k in range(outer):
+                work[k, at, :inner], work[k, at, inner:] = twiddled(real[k], imag[k], tw, k)
+
+    if not last:
+        row_out(mat_next, work, out)
+
+
+def call(body, shape, work, micros, *operands, scalars=0):
+    in_specs = [pl.BlockSpec(memory_space=pltpu.SMEM)] * scalars
+    in_specs += [pl.BlockSpec(memory_space=pltpu.VMEM)] * (len(operands) - scalars)
+    return pl.pallas_call(
+        body,
+        out_shape=jax.ShapeDtypeStruct(shape, jnp.float32),
+        in_specs=in_specs,
+        out_specs=pl.BlockSpec(memory_space=pltpu.VMEM),
+        scratch_shapes=[pltpu.VMEM(work, jnp.float32)] if work else [],
+        compiler_params=pltpu.CompilerParams(vmem_limit_bytes=VMEM_LIMIT),
+        cost_estimate=pl.CostEstimate(flops=int(micros * 4e8), bytes_accessed=int(micros * 3e6), transcendentals=0),
+    )(*operands)
+
+
+def shards(wavefield, freqs, velocity, ref_slow):
+    slabs = lax.axis_size("slab")
+    slab_index = lax.axis_index("slab")
+    rows = wavefield.shape[2]
+    width_x = rows * slabs
+    width_y = wavefield.shape[3]
+    columns = width_y // slabs
+    depth = ref_slow.shape[0]
+    across = (slabs, 2, rows, columns)
+    row_fwd = matrix_of(columns, width_y, -1, False)
+    row_inv = matrix_of(columns, width_y, 1, False)
+    col_fwd = matrix_of(rows, width_x, -1, True)
+    col_inv = matrix_of(rows, width_x, 1, True)
+    row_tw = twiddle_table(slabs, columns, False)
+    col_tw = twiddle_table(slabs, rows, True)
+    row_work = (slabs, rows, 2 * columns)
+
+    number = slab_index + slabs * jnp.arange(columns, dtype=jnp.int32)
+    number = jnp.where(number < width_y // 2, number, number - width_y)
+    along_y = number.astype(jnp.float32) / width_y
+    fy2 = jnp.broadcast_to((along_y * along_y)[None, :], (ROWS, columns))
+
+    def exchange(x):
+        return lax.all_to_all(x, "slab", split_axis=0, concat_axis=0, tiled=True)
+
+    freq_count = lax.axis_size("freq")
+    tiles = jnp.broadcast_to(velocity[None], (freq_count,) + velocity.shape)
+    tiles = lax.all_to_all(tiles, "freq", split_axis=0, concat_axis=0, tiled=True)
+
+    part_send = call(first_kernel, across, row_work, 4, wavefield[:, 0], row_fwd, row_tw)
+    for level in range(depth):
+        last = level == depth - 1
+        scal = jnp.concatenate([freqs, ref_slow[level]])
+        got = exchange(part_send)
+        shift = call(
+            functools.partial(spread_kernel, slabs, width_x), (2,) + across, None, 8, scal, fy2, scalars=1
+        )
+        tile = jnp.concatenate([tiles[i, level] for i in range(freq_count)], axis=1)
+        weight = call(weight_kernel, (2, 2, rows, width_y), None, 8, scal, tile, scalars=1)
+        spec = call(column_forward_kernel, across, across, 4, got, col_fwd, col_tw)
+        back = []
+        for branch in range(2):
+            sent = call(column_back_kernel, across, across, 4, spec, shift[branch], col_inv, col_tw)
+            back.append(exchange(sent))
+        part = call(row_back_kernel, (2, rows, width_y), row_work, 4, back[0], weight[0], row_inv, row_tw)
+        part_send = call(
+            functools.partial(row_join_kernel, last),
+            (2, rows, width_y) if last else across,
+            row_work, 5, back[1], weight[1], part, row_inv, row_tw, row_fwd,
+        )
+    return part_send[:, None]
+
+
 def solution(mesh):
-    return jax.shard_map(
-        shards,
-        mesh=mesh,
-        in_specs=(P(None, "freq", "slab", None), P("freq"), P(None, "slab", "freq"), P()),
-        out_specs=P(None, "freq", "slab", None),
-        check_vma=False,
-    )
+    slabs = mesh.shape["slab"]
+
+    def program(wavefield, freqs, velocity, ref_slow):
+        width_x, width_y = wavefield.shape[2:]
+        whole_tiles = (
+            width_y // slabs == LANES
+            and width_x // slabs == LANES
+            and wavefield.shape[1] == mesh.shape["freq"]
+        )
+        return jax.shard_map(
+            shards if whole_tiles else shards_generic,
+            mesh=mesh,
+            in_specs=(P(None, "freq", "slab", None), P("freq"), P(None, "slab", "freq"), P()),
+            out_specs=P(None, "freq", "slab", None),
+            check_vma=False,
+        )(wavefield, freqs, velocity, ref_slow)
+
+    return program

time: 794 us -> 583 us (0.73)
  matrix products: 223 us -> 0 us
  Pallas kernels: 0 us -> 157 us
  local copies, waits for them, and re-layouts: 167 us -> 38 us
  other arithmetic: 75.2 us -> 3.93 us
  blocking collectives: 0 us -> 54 us
  waiting for transfers between devices: 251 us -> 285 us
  loops' own time: 14.6 us -> 0 us
  between operations: 14.1 us -> 0.72 us
    dot_general x144 -> x0, matrix products: 223 us -> none  [product(): return jnp.einsum(form, matrix, data, precision=lax.Precision.HIGHEST)]
    pallas_call x0 -> x22, Pallas kernels: none -> 157 us  [call(): pl.pallas_call(body, out_shape=jax.ShapeDtypeStruct(shape, jnp.float32),...]
    another operation x24 -> x0, local copies, waits for them, and re-layouts: 76.4 us -> none  [the longest x6 60.7 us: advance(): shifted.append(jnp.stack((back_real, back_imag)))]
    all_to_all x0 -> x1, blocking collectives: none -> 54 us  [exchange(): return lax.all_to_all(x, 'slab', split_axis=0, concat_axis=0, tiled=True)]
    another operation x15 -> x0, other arithmetic: 44.1 us -> none  [the longest x6 33.4 us: advance(): return jnp.stack((new_real, new_imag))]
    all_to_all x15 -> x0, local copies, waits for them, and re-layouts: 35.7 us -> none  [the longest x12 29.5 us: advance(): lax.all_to_all(shifted[branch], 'slab', split_axis=2, concat_axis=3, tile...]
    all_to_all x9, waiting for transfers between devices: 251 us -> 285 us  [the longest x8 277 us: exchange(): return lax.all_to_all(x, 'slab', split_axis=0, concat_axis=0, tiled=True)]
    select_n x3 -> x0, other arithmetic: 30.7 us -> none  [advance(): prop_imag = jnp.where(live, jnp.sin(angle), jnp.zeros_like(angle))]
  transfers between devices with their start and end apart: 12 -> 9, of which waited for: 9 -> 9; matrix products, arithmetic and copies ran while one was open for 31% -> 6% of each run, Pallas kernels for 0% -> 16%
where the time goes in v1:
time: 583 us; the launch traced here: 582 us
  waiting for transfers between devices  285 us (49%)
  Pallas kernels  157 us (27%)
  blocking collectives  54 us (9%)
  starting transfers between devices  43.4 us (7%)
  local copies, waits for them, and re-layouts  38 us (7%)
    all_to_all x8, waiting for transfers between devices, exchange(): return lax.all_to_all(x, 'slab', split_axis=0, concat_axis=0, tiled=True)  277 us
    pallas_call x22, Pallas kernels, call(): pl.pallas_call(body, out_shape=jax.ShapeDtypeStruct(shape, jnp.float32),...  157 us
    all_to_all x1, blocking collectives, exchange(): return lax.all_to_all(x, 'slab', split_axis=0, concat_axis=0, tiled=True)  54 us
    all_to_all x8, starting transfers between devices, exchange(): return lax.all_to_all(x, 'slab', split_axis=0, concat_axis=0, tiled=True)  39.3 us
    squeeze x3, local copies, waits for them, and re-layouts, shards(): weight[0]  14.2 us
    squeeze x3, local copies, waits for them, and re-layouts, shards(): shift[branch]  14.2 us
  transfers between devices with their start and end apart: 9, of which 9 were waited for; matrix products, arithmetic and copies ran while one was open for 6% of the time, Pallas kernels for 16%

profile of v1, /device:TPU:11, one launch (start us, length us, event | category | flops | bytes accessed | tf_op | source)
XLA Modules:
  0.0 582.0 jit_solution(401415488225665909)
XLA Ops:
  5.9 54.0 %all_to_all.50.got = f32[16,2,128,128]{3,2,1,0:T(8,128)} all-to-all(f32[16,2,128,128]{3,2,1,0:T(8,128)} %shard_map.100), channel_id=1, replica_groups=mesh['freq'=2,'slab'=16] {'slab'}, dimensions={0} | all-to-all | bytes 4194304 | tf_op jit(solution)/shard_map/all_to_all | solution.py:487
  68.2 7.2 %shard_map.102 = f32[2,16,2,128,128]{4,3,2,1,0:T(8,128)} custom-call(f32[3]{0:T(128)} %get-tuple-element.26.scal, f32[8,128]{1,0:T(8,128)} %broadcast_in_dim.6.fy2), custom_call_target="tpu_custom_call" | custom-call | flops 3200000000 | bytes 24000000 | tf_op jit(solution)/shard_map/pallas_call | solution.py:453
  86.9 7.4 %shard_map.105 = f32[16,2,128,128]{3,2,1,0:T(8,128)} custom-call(f32[16,2,128,128]{3,2,1,0:T(8,128)} %shard_map.101.spec, f32[16,2,128,128]{3,2,1,0:T(8,128)} %get-tuple-element.18.shift, bf16[2,256,256]{2,1,0:T(8,128)(2,1)} %constant.22.clone.mat.mat_next, f32[16,2,128,128]{3,2,1,0:T(8,128)} %constant.25.clone.tw), custom_call_target="tpu_custom_call" | custom-call | flops 1600000000 | bytes 12000000 | tf_op jit(solution)/shard_map/pallas_call | solution.py:453
  94.3 7.9 %all-to-all-done.2 = f32[2,3,128,1024]{3,2,1,0:T(8,128)S(1)} async-done(((f32[2,3,128,1024]{3,2,1,0:T(8,128)}), f32[2,3,128,1024]{3,2,1,0:T(8,128)S(1)}, u32[]{:S(2)}, u32[]{:S(2)}) %all-to-all-start.2) | async-done | bytes 3145760 | tf_op jit(solution)/shard_map/all_to_all | solution.py:491
  108.0 7.4 %shard_map.103 = f32[16,2,128,128]{3,2,1,0:T(8,128)} custom-call(f32[16,2,128,128]{3,2,1,0:T(8,128)} %shard_map.101.spec, f32[16,2,128,128]{3,2,1,0:T(8,128)} %get-tuple-element.19.shift, bf16[2,256,256]{2,1,0:T(8,128)(2,1)} %constant.22.clone.mat.mat_next, f32[16,2,128,128]{3,2,1,0:T(8,128)} %constant.25.clone.tw), custom_call_target="tpu_custom_call" | custom-call | flops 1600000000 | bytes 12000000 | tf_op jit(solution)/shard_map/pallas_call | solution.py:453
  115.4 40.1 %all-to-all-done.3.got = f32[16,2,128,128]{3,2,1,0:T(8,128)} async-done(((f32[16,2,128,128]{3,2,1,0:T(8,128)}), f32[16,2,128,128]{3,2,1,0:T(8,128)}, u32[]{:S(2)}, u32[]{:S(2)}) %all-to-all-start.3) | async-done | bytes 2097184 | tf_op jit(solution)/shard_map/all_to_all | solution.py:487
  180.5 27.4 %all-to-all-done.1.got = f32[16,2,128,128]{3,2,1,0:T(8,128)} async-done(((f32[16,2,128,128]{3,2,1,0:T(8,128)}), f32[16,2,128,128]{3,2,1,0:T(8,128)}, u32[]{:S(2)}, u32[]{:S(2)}) %all-to-all-start.1) | async-done | bytes 2097184 | tf_op jit(solution)/shard_map/all_to_all | solution.py:487
  207.8 10.0 %shard_map.107 = f32[16,2,128,128]{3,2,1,0:T(8,128)} custom-call(f32[16,2,128,128]{3,2,1,0:T(8,128)} %all-to-all-done.1.got, f32[2,128,2048]{2,1,0:T(8,128)} %get-tuple-element.17.weight, f32[2,128,2048]{2,1,0:T(8,128)} %shard_map.106.part, bf16[2,256,256]{2,1,0:T(8,128)(2,1)} %constant.24.clone.mat, f32[16,2,8,128]{3,2,1,0:T(8,128)} %constant.23.clone.tw, ...), custom_call_target="tpu_custom_call" | custom-call | flops 2000000000 | bytes 15000000 | tf_op jit(solution)/shard_map/pallas_call | solution.py:453
  222.6 7.2 %shard_map.109 = f32[2,16,2,128,128]{4,3,2,1,0:T(8,128)} custom-call(f32[3]{0:T(128)} %get-tuple-element.27.scal, f32[8,128]{1,0:T(8,128)} %broadcast_in_dim.6.fy2), custom_call_target="tpu_custom_call" | custom-call | flops 3200000000 | bytes 24000000 | tf_op jit(solution)/shard_map/pallas_call | solution.py:453
  234.6 35.5 %all-to-all-done.4.got = f32[16,2,128,128]{3,2,1,0:T(8,128)S(1)} async-done(((f32[16,2,128,128]{3,2,1,0:T(8,128)}), f32[16,2,128,128]{3,2,1,0:T(8,128)S(1)}, u32[]{:S(2)}, u32[]{:S(2)}) %all-to-all-start.4) | async-done | bytes 2097184 | tf_op jit(solution)/shard_map/all_to_all | solution.py:487
  271.3 6.7 %shard_map.108.spec = f32[16,2,128,128]{3,2,1,0:T(8,128)} custom-call(f32[16,2,128,128]{3,2,1,0:T(8,128)} %copy-done.3, bf16[2,256,256]{2,1,0:T(8,128)(2,1)} %constant.24.clone.mat, f32[16,2,128,128]{3,2,1,0:T(8,128)} %constant.25.clone.tw), custom_call_target="tpu_custom_call" | custom-call | flops 1600000000 | bytes 12000000 | tf_op jit(solution)/shard_map/pallas_call | solution.py:453
  278.0 7.3 %shard_map.112 = f32[16,2,128,128]{3,2,1,0:T(8,128)} custom-call(f32[16,2,128,128]{3,2,1,0:T(8,128)} %shard_map.108.spec, f32[16,2,128,128]{3,2,1,0:T(8,128)} %get-tuple-element.14.shift, bf16[2,256,256]{2,1,0:T(8,128)(2,1)} %constant.22.clone.mat.mat_next, f32[16,2,128,128]{3,2,1,0:T(8,128)} %constant.25.clone.tw), custom_call_target="tpu_custom_call" | custom-call | flops 1600000000 | bytes 12000000 | tf_op jit(solution)/shard_map/pallas_call | solution.py:453
  290.2 7.3 %shard_map.110 = f32[16,2,128,128]{3,2,1,0:T(8,128)} custom-call(f32[16,2,128,128]{3,2,1,0:T(8,128)} %shard_map.108.spec, f32[16,2,128,128]{3,2,1,0:T(8,128)} %get-tuple-element.15.shift, bf16[2,256,256]{2,1,0:T(8,128)(2,1)} %constant.22.clone.mat.mat_next, f32[16,2,128,128]{3,2,1,0:T(8,128)} %constant.25.clone.tw), custom_call_target="tpu_custom_call" | custom-call | flops 1600000000 | bytes 12000000 | tf_op jit(solution)/shard_map/pallas_call | solution.py:453
  297.5 40.1 %all-to-all-done.6.got = f32[16,2,128,128]{3,2,1,0:T(8,128)S(1)} async-done(((f32[16,2,128,128]{3,2,1,0:T(8,128)}), f32[16,2,128,128]{3,2,1,0:T(8,128)S(1)}, u32[]{:S(2)}, u32[]{:S(2)}) %all-to-all-start.6) | async-done | bytes 2097184 | tf_op jit(solution)/shard_map/all_to_all | solution.py:487
  361.2 30.1 %all-to-all-done.5.got = f32[16,2,128,128]{3,2,1,0:T(8,128)} async-done(((f32[16,2,128,128]{3,2,1,0:T(8,128)}), f32[16,2,128,128]{3,2,1,0:T(8,128)}, u32[]{:S(2)}, u32[]{:S(2)}) %all-to-all-start.5) | async-done | bytes 2097184 | tf_op jit(solution)/shard_map/all_to_all | solution.py:487
  391.3 10.0 %shard_map.114 = f32[16,2,128,128]{3,2,1,0:T(8,128)} custom-call(f32[16,2,128,128]{3,2,1,0:T(8,128)} %all-to-all-done.5.got, f32[2,128,2048]{2,1,0:T(8,128)} %get-tuple-element.13.weight, f32[2,128,2048]{2,1,0:T(8,128)} %shard_map.113.part, bf16[2,256,256]{2,1,0:T(8,128)(2,1)} %constant.24.clone.mat, f32[16,2,8,128]{3,2,1,0:T(8,128)} %constant.23.clone.tw, ...), custom_call_target="tpu_custom_call" | custom-call | flops 2000000000 | bytes 15000000 | tf_op jit(solution)/shard_map/pallas_call | solution.py:453
  406.6 7.2 %shard_map.116 = f32[2,16,2,128,128]{4,3,2,1,0:T(8,128)} custom-call(f32[3]{0:T(128)} %pad_maximum_fusion.5.scal, f32[8,128]{1,0:T(8,128)} %broadcast_in_dim.6.fy2), custom_call_target="tpu_custom_call" | custom-call | flops 3200000000 | bytes 24000000 | tf_op jit(solution)/shard_map/pallas_call | solution.py:453
  418.6 34.9 %all-to-all-done.7.got = f32[16,2,128,128]{3,2,1,0:T(8,128)S(1)} async-done(((f32[16,2,128,128]{3,2,1,0:T(8,128)}), f32[16,2,128,128]{3,2,1,0:T(8,128)S(1)}, u32[]{:S(2)}, u32[]{:S(2)}) %all-to-all-start.7) | async-done | bytes 2097184 | tf_op jit(solution)/shard_map/all_to_all | solution.py:487
  454.8 6.7 %shard_map.115.spec = f32[16,2,128,128]{3,2,1,0:T(8,128)} custom-call(f32[16,2,128,128]{3,2,1,0:T(8,128)} %copy-done.2, bf16[2,256,256]{2,1,0:T(8,128)(2,1)} %constant.24.clone.mat, f32[16,2,128,128]{3,2,1,0:T(8,128)} %constant.25.clone.tw), custom_call_target="tpu_custom_call" | custom-call | flops 1600000000 | bytes 12000000 | tf_op jit(solution)/shard_map/pallas_call | solution.py:453
  461.5 7.3 %shard_map.119 = f32[16,2,128,128]{3,2,1,0:T(8,128)} custom-call(f32[16,2,128,128]{3,2,1,0:T(8,128)} %shard_map.115.spec, f32[16,2,128,128]{3,2,1,0:T(8,128)} %get-tuple-element.10.shift, bf16[2,256,256]{2,1,0:T(8,128)(2,1)} %constant.22.clone.mat.mat_next, f32[16,2,128,128]{3,2,1,0:T(8,128)} %constant.25.clone.tw), custom_call_target="tpu_custom_call" | custom-call | flops 1600000000 | bytes 12000000 | tf_op jit(solution)/shard_map/pallas_call | solution.py:453
  473.6 7.3 %shard_map.117 = f32[16,2,128,128]{3,2,1,0:T(8,128)} custom-call(f32[16,2,128,128]{3,2,1,0:T(8,128)} %shard_map.115.spec, f32[16,2,128,128]{3,2,1,0:T(8,128)} %get-tuple-element.11.shift, bf16[2,256,256]{2,1,0:T(8,128)(2,1)} %constant.22.clone.mat.mat_next, f32[16,2,128,128]{3,2,1,0:T(8,128)} %constant.25.clone.tw), custom_call_target="tpu_custom_call" | custom-call | flops 1600000000 | bytes 12000000 | tf_op jit(solution)/shard_map/pallas_call | solution.py:453
  480.9 40.1 %all-to-all-done.9.got = f32[16,2,128,128]{3,2,1,0:T(8,128)S(1)} async-done(((f32[16,2,128,128]{3,2,1,0:T(8,128)}), f32[16,2,128,128]{3,2,1,0:T(8,128)S(1)}, u32[]{:S(2)}, u32[]{:S(2)}) %all-to-all-start.9) | async-done | bytes 2097184 | tf_op jit(solution)/shard_map/all_to_all | solution.py:487
  545.8 28.9 %all-to-all-done.8.got = f32[16,2,128,128]{3,2,1,0:T(8,128)} async-done(((f32[16,2,128,128]{3,2,1,0:T(8,128)}), f32[16,2,128,128]{3,2,1,0:T(8,128)}, u32[]{:S(2)}, u32[]{:S(2)}) %all-to-all-start.8) | async-done | bytes 2097184 | tf_op jit(solution)/shard_map/all_to_all | solution.py:487
  574.7 7.3 %shard_map.121 = f32[2,128,2048]{2,1,0:T(8,128)} custom-call(f32[16,2,128,128]{3,2,1,0:T(8,128)} %all-to-all-done.8.got, f32[2,128,2048]{2,1,0:T(8,128)} %get-tuple-element.9.weight, f32[2,128,2048]{2,1,0:T(8,128)} %shard_map.120.part, bf16[2,256,256]{2,1,0:T(8,128)(2,1)} %constant.24.clone.mat, f32[16,2,8,128]{3,2,1,0:T(8,128)} %constant.23.clone.tw, ...), custom_call_target="tpu_custom_call" | custom-call | flops 2000000000 | bytes 15000000 | tf_op jit(solution)/shard_map/pallas_call | solution.py:453
  (48 shorter events, 136.0 us)
Async XLA Ops:
  5.9 54.0 %copy-start.6 = (f32[3,128,1024]{2,1,0:T(8,128)S(1)}, f32[3,128,1024]{2,1,0:T(8,128)}, u32[]{:S(2)}) copy-start(f32[3,128,1024]{2,1,0:T(8,128)} %param.12) | copy-start | bytes 4718596
  62.0 4.8 copy-start.7
  62.0 40.1 %all-to-all-start.2 = ((f32[2,3,128,1024]{3,2,1,0:T(8,128)}), f32[2,3,128,1024]{3,2,1,0:T(8,128)S(1)}, u32[]{:S(2)}, u32[]{:S(2)}) async-start(f32[2,3,128,1024]{3,2,1,0:T(8,128)} %broadcast_in_dim.7), calls=%async_computation.2 | async-start | bytes 6291456 | tf_op jit(solution)/shard_map/all_to_all | solution.py:491
  102.1 53.4 %all-to-all-start.3 = ((f32[16,2,128,128]{3,2,1,0:T(8,128)}), f32[16,2,128,128]{3,2,1,0:T(8,128)}, u32[]{:S(2)}, u32[]{:S(2)}) async-start(f32[16,2,128,128]{3,2,1,0:T(8,128)} %shard_map.105), calls=%async_computation.3 | async-start | bytes 4194304 | tf_op jit(solution)/shard_map/all_to_all | solution.py:487
  155.5 52.3 %all-to-all-start.1 = ((f32[16,2,128,128]{3,2,1,0:T(8,128)}), f32[16,2,128,128]{3,2,1,0:T(8,128)}, u32[]{:S(2)}, u32[]{:S(2)}) async-start(f32[16,2,128,128]{3,2,1,0:T(8,128)} %shard_map.103), calls=%async_computation.1 | async-start | bytes 4194304 | tf_op jit(solution)/shard_map/all_to_all | solution.py:487
  217.8 52.2 %all-to-all-start.4 = ((f32[16,2,128,128]{3,2,1,0:T(8,128)}), f32[16,2,128,128]{3,2,1,0:T(8,128)S(1)}, u32[]{:S(2)}, u32[]{:S(2)}) async-start(f32[16,2,128,128]{3,2,1,0:T(8,128)} %shard_map.107), calls=%async_computation.4 | async-start | bytes 4194304 | tf_op jit(solution)/shard_map/all_to_all | solution.py:487
  270.0 1.3 copy-start.3
  285.4 52.2 %all-to-all-start.6 = ((f32[16,2,128,128]{3,2,1,0:T(8,128)}), f32[16,2,128,128]{3,2,1,0:T(8,128)S(1)}, u32[]{:S(2)}, u32[]{:S(2)}) async-start(f32[16,2,128,128]{3,2,1,0:T(8,128)} %shard_map.112), calls=%async_computation.6 | async-start | bytes 4194304 | tf_op jit(solution)/shard_map/all_to_all | solution.py:487
  337.6 1.4 copy-start.1
  339.0 52.3 %all-to-all-start.5 = ((f32[16,2,128,128]{3,2,1,0:T(8,128)}), f32[16,2,128,128]{3,2,1,0:T(8,128)}, u32[]{:S(2)}, u32[]{:S(2)}) async-start(f32[16,2,128,128]{3,2,1,0:T(8,128)} %shard_map.110), calls=%async_computation.5 | async-start | bytes 4194304 | tf_op jit(solution)/shard_map/all_to_all | solution.py:487
  401.3 52.2 %all-to-all-start.7 = ((f32[16,2,128,128]{3,2,1,0:T(8,128)}), f32[16,2,128,128]{3,2,1,0:T(8,128)S(1)}, u32[]{:S(2)}, u32[]{:S(2)}) async-start(f32[16,2,128,128]{3,2,1,0:T(8,128)} %shard_map.114), calls=%async_computation.7 | async-start | bytes 4194304 | tf_op jit(solution)/shard_map/all_to_all | solution.py:487
  453.5 1.3 copy-start.2
  468.8 52.2 %all-to-all-start.9 = ((f32[16,2,128,128]{3,2,1,0:T(8,128)}), f32[16,2,128,128]{3,2,1,0:T(8,128)S(1)}, u32[]{:S(2)}, u32[]{:S(2)}) async-start(f32[16,2,128,128]{3,2,1,0:T(8,128)} %shard_map.119), calls=%async_computation.9 | async-start | bytes 4194304 | tf_op jit(solution)/shard_map/all_to_all | solution.py:487
  480.9 46.2 %copy-start.4 = (f32[128,1024]{1,0:T(8,128)S(1)}, f32[128,1024]{1,0:T(8,128)}, u32[]{:S(2)}) copy-start(f32[128,1024]{1,0:T(8,128)} %get-tuple-element.20) | copy-start | bytes 1572868
  480.9 46.2 %copy-start.5 = (f32[128,1024]{1,0:T(8,128)S(1)}, f32[128,1024]{1,0:T(8,128)}, u32[]{:S(2)}) copy-start(f32[128,1024]{1,0:T(8,128)} %get-tuple-element.21) | copy-start | bytes 1572868
  521.0 1.4 copy-start
  522.4 52.3 %all-to-all-start.8 = ((f32[16,2,128,128]{3,2,1,0:T(8,128)}), f32[16,2,128,128]{3,2,1,0:T(8,128)}, u32[]{:S(2)}, u32[]{:S(2)}) async-start(f32[16,2,128,128]{3,2,1,0:T(8,128)} %shard_map.117), calls=%async_computation.8 | async-start | bytes 4194304 | tf_op jit(solution)/shard_map/all_to_all | solution.py:487

commit v2 on v1

--- a/solution.py
+++ b/solution.py
@@ -252,9 +252,9 @@
     return horner(COS_TERMS, z), rest * horner(SIN_TERMS, z)
 
 
-def spread_kernel(outer, length, scal, fy2, out):
+def spread_kernel(outer, length, scal, fy2, *outs):
     freq = scal[0]
-    rows = out.shape[3]
+    rows = outs[0].shape[2]
 
     @pl.loop(0, outer)
     def _(k1):
@@ -272,25 +272,30 @@
                 live = target >= 0
                 cosine, sine = circle(turns)
                 decay = jnp.exp(turns * (-two_pi))
-                out[branch, k1, 0, pl.ds(base, 32), :] = jnp.where(live, cosine, decay)
-                out[branch, k1, 1, pl.ds(base, 32), :] = jnp.where(live, sine, 0.0)
-
-
-def weight_kernel(scal, velocity, out):
+                outs[branch][k1, 0, pl.ds(base, 32), :] = jnp.where(live, cosine, decay)
+                outs[branch][k1, 1, pl.ds(base, 32), :] = jnp.where(live, sine, 0.0)
+
+
+def weight_kernel(scal, order, *refs):
+    tiles, outs = refs[:-2], refs[-2:]
     freq = scal[0]
-    rows, width = velocity.shape
+    rows, part = tiles[0].shape
+    width = part * len(tiles)
 
     @pl.loop(0, rows // ROWS)
     def _(c):
         at = pl.ds(pl.multiple_of(c * ROWS, ROWS), ROWS)
         for j in range(width // 512):
             cols = slice(j * 512, (j + 1) * 512)
-            slowness = 1.0 / velocity[at, cols]
+            first = j * 512 // part
+            inside = slice(j * 512 - first * part, (j + 1) * 512 - first * part)
+            here, there = tiles[first][at, inside], tiles[1 - first][at, inside]
+            slowness = 1.0 / jnp.where(order[0] == 0, here, there)
             upper = jnp.clip((slowness - scal[1]) / (scal[2] - scal[1]), 0.0, 1.0)
             for branch, weight in enumerate((1.0 - upper, upper)):
                 cosine, sine = circle(depth_step * freq * (slowness - scal[1 + branch]))
-                out[branch, 0, at, cols] = weight * cosine
-                out[branch, 1, at, cols] = weight * sine
+                outs[branch][0, at, cols] = weight * cosine
+                outs[branch][1, at, cols] = weight * sine
 
 
 def row_out(mat, work, out):
@@ -447,14 +452,16 @@
         row_out(mat_next, work, out)
 
 
-def call(body, shape, work, micros, *operands, scalars=0):
+def call(body, shape, work, micros, *operands, scalars=0, outputs=1):
     in_specs = [pl.BlockSpec(memory_space=pltpu.SMEM)] * scalars
     in_specs += [pl.BlockSpec(memory_space=pltpu.VMEM)] * (len(operands) - scalars)
+    result = jax.ShapeDtypeStruct(shape, jnp.float32)
+    spec = pl.BlockSpec(memory_space=pltpu.VMEM)
     return pl.pallas_call(
         body,
-        out_shape=jax.ShapeDtypeStruct(shape, jnp.float32),
+        out_shape=result if outputs == 1 else (result,) * outputs,
         in_specs=in_specs,
-        out_specs=pl.BlockSpec(memory_space=pltpu.VMEM),
+        out_specs=spec if outputs == 1 else (spec,) * outputs,
         scratch_shapes=[pltpu.VMEM(work, jnp.float32)] if work else [],
         compiler_params=pltpu.CompilerParams(vmem_limit_bytes=VMEM_LIMIT),
         cost_estimate=pl.CostEstimate(flops=int(micros * 4e8), bytes_accessed=int(micros * 3e6), transcendentals=0),
@@ -478,40 +485,84 @@
     col_tw = twiddle_table(slabs, rows, True)
     row_work = (slabs, rows, 2 * columns)
 
-    number = slab_index + slabs * jnp.arange(columns, dtype=jnp.int32)
+    freq_count = lax.axis_size("freq")
+    group = slabs // freq_count
+    run = group // freq_count
+    row = lax.axis_index("freq")
+    both = ("freq", "slab")
+    everyone = [(y, s) for y in range(freq_count) for s in range(slabs)]
+
+    def owner(slab):
+        return (slab // run) % freq_count, (slab // group) * run + slab % run
+
+    def device(y, g, place):
+        return y * slabs + g * group + place
+
+    members = []
+    for g in range(freq_count):
+        members.append([device(y, g, place) for y, place in map(owner, range(slabs))])
+    here = lax.rem(slab_index, group)
+    mine = (here // run) * group + row * run + lax.rem(here, run)
+
+    def swap(x, name):
+        return lax.all_to_all(x, name, split_axis=0, concat_axis=0, tiled=True)
+
+    def exchange(x):
+        return lax.all_to_all(x, both, split_axis=0, concat_axis=0, tiled=True, axis_index_groups=members)
+
+    home = [(y * slabs + s, (s // group) * slabs + y * group + s % group) for y, s in everyone]
+    group_freq = lax.ppermute(freqs, both, home)
+
+    number = mine + slabs * jnp.arange(columns, dtype=jnp.int32)
     number = jnp.where(number < width_y // 2, number, number - width_y)
     along_y = number.astype(jnp.float32) / width_y
     fy2 = jnp.broadcast_to((along_y * along_y)[None, :], (ROWS, columns))
 
-    def exchange(x):
-        return lax.all_to_all(x, "slab", split_axis=0, concat_axis=0, tiled=True)
-
-    freq_count = lax.axis_size("freq")
-    tiles = jnp.broadcast_to(velocity[None], (freq_count,) + velocity.shape)
-    tiles = lax.all_to_all(tiles, "freq", split_axis=0, concat_axis=0, tiled=True)
-
     part_send = call(first_kernel, across, row_work, 4, wavefield[:, 0], row_fwd, row_tw)
+    sends = part_send.reshape(freq_count, freq_count, run, 2, rows, columns)
+    sends = sends.swapaxes(0, 1).reshape(across)
+    got = swap(swap(sends, "freq"), "slab")
+
+    def grouped_velocity(level):
+        moved = []
+        for shift in range(freq_count):
+            route = []
+            for y, s in everyone:
+                to_row, place = owner(s)
+                route.append((y * slabs + s, device(to_row, (to_row + y + shift) % freq_count, place)))
+            moved.append(lax.ppermute(velocity[level], both, route))
+        return moved
+
+    order = ((slab_index // group + freq_count - row) % freq_count).astype(jnp.int32)[None]
+
     for level in range(depth):
         last = level == depth - 1
-        scal = jnp.concatenate([freqs, ref_slow[level]])
-        got = exchange(part_send)
+        if level:
+            got = exchange(part_send)
+        with jax.named_scope(f"vel{level}"):
+            tiles = grouped_velocity(level)
+        scal = jnp.concatenate([group_freq, ref_slow[level]])
         shift = call(
-            functools.partial(spread_kernel, slabs, width_x), (2,) + across, None, 8, scal, fy2, scalars=1
+            functools.partial(spread_kernel, slabs, width_x), across, None, 8, scal, fy2, scalars=1, outputs=2
         )
-        tile = jnp.concatenate([tiles[i, level] for i in range(freq_count)], axis=1)
-        weight = call(weight_kernel, (2, 2, rows, width_y), None, 8, scal, tile, scalars=1)
-        spec = call(column_forward_kernel, across, across, 4, got, col_fwd, col_tw)
+        weight = call(weight_kernel, (2, rows, width_y), None, 8, scal, order, *tiles, scalars=2, outputs=2)
+        spec = call(column_forward_kernel, across, across, 7, got, col_fwd, col_tw)
         back = []
         for branch in range(2):
-            sent = call(column_back_kernel, across, across, 4, spec, shift[branch], col_inv, col_tw)
-            back.append(exchange(sent))
-        part = call(row_back_kernel, (2, rows, width_y), row_work, 4, back[0], weight[0], row_inv, row_tw)
+            sent = call(column_back_kernel, across, across, 7, spec, shift[branch], col_inv, col_tw)
+            with jax.named_scope(f"back{level}_{branch}"):
+                back.append(exchange(sent))
+        part = call(row_back_kernel, (2, rows, width_y), row_work, 6, back[0], weight[0], row_inv, row_tw)
         part_send = call(
             functools.partial(row_join_kernel, last),
             (2, rows, width_y) if last else across,
-            row_work, 5, back[1], weight[1], part, row_inv, row_tw, row_fwd,
+            row_work, 9, back[1], weight[1], part, row_inv, row_tw, row_fwd,
         )
-    return part_send[:, None]
+    leave = []
+    for y, s in everyone:
+        to_row, place = owner(s)
+        leave.append((device(to_row, y, place), y * slabs + s))
+    return lax.ppermute(part_send, both, leave)[:, None]
 
 
 def solution(mesh):
@@ -522,7 +573,8 @@
         whole_tiles = (
             width_y // slabs == LANES
             and width_x // slabs == LANES
-            and wavefield.shape[1] == mesh.shape["freq"]
+            and wavefield.shape[1] == mesh.shape["freq"] == 2
+            and slabs % 4 == 0
         )
         return jax.shard_map(
             shards if whole_tiles else shards_generic,

time: 583 us -> 586 us (level)
  starting transfers between devices: 43.4 us -> 101 us
  blocking collectives: 54 us -> 27.6 us
  local copies, waits for them, and re-layouts: 38 us -> 15.7 us
  waiting for transfers between devices: 285 us -> 274 us
    all_to_all x9, waiting for transfers between devices: 285 us -> 132 us  [the longest x8 95.6 us: exchange(): lax.all_to_all(x, both, split_axis=0, concat_axis=0, tiled=True, axis_ind...]
    ppermute x0 -> x8, waiting for transfers between devices: none -> 142 us  [the longest x6 97.9 us: grouped_velocity(): moved.append(lax.ppermute(velocity[level], both, route))]
    all_to_all x9, starting transfers between devices: 43.4 us -> 77.8 us  [the longest x8 70.3 us: exchange(): lax.all_to_all(x, both, split_axis=0, concat_axis=0, tiled=True, axis_ind...]
    squeeze x7 -> x1, local copies, waits for them, and re-layouts: 29.7 us -> 1.46 us  [grouped_velocity(): moved.append(lax.ppermute(velocity[level], both, route))]
    all_to_all x1, blocking collectives: 54 us -> 27.6 us  [swap(): return lax.all_to_all(x, name, split_axis=0, concat_axis=0, tiled=True)]
    ppermute x0 -> x8, starting transfers between devices: none -> 23.2 us  [the longest x6 16.3 us: grouped_velocity(): moved.append(lax.ppermute(velocity[level], both, route))]
    unnamed x16 -> x27, local copies, waits for them, and re-layouts: 5.44 us -> 11.7 us
  transfers between devices with their start and end apart: 9 -> 17, of which waited for: 9 -> 13; matrix products, arithmetic and copies ran while one was open for 6% -> 1% of each run, Pallas kernels for 16% -> 14%
where the time goes in v2:
time: 586 us; the launch traced here: 580 us
  waiting for transfers between devices  274 us (47%)
  Pallas kernels  158 us (27%)
  starting transfers between devices  101 us (17%)
  blocking collectives  27.6 us (5%)
  local copies, waits for them, and re-layouts  15.7 us (3%)
    pallas_call x22, Pallas kernels, call(): pl.pallas_call(body, out_shape=result if outputs == 1 else (result,) * ou...  158 us
    ppermute x6, waiting for transfers between devices, grouped_velocity(): moved.append(lax.ppermute(velocity[level], both, route))  97.9 us
    all_to_all x8, waiting for transfers between devices, exchange(): lax.all_to_all(x, both, split_axis=0, concat_axis=0, tiled=True, axis_ind...  95.6 us
    all_to_all x8, starting transfers between devices, exchange(): lax.all_to_all(x, both, split_axis=0, concat_axis=0, tiled=True, axis_ind...  70.3 us
    ppermute x1, waiting for transfers between devices, shards(): return lax.ppermute(part_send, both, leave)[:, None]  44.3 us
    all_to_all x1, waiting for transfers between devices, swap(): return lax.all_to_all(x, name, split_axis=0, concat_axis=0, tiled=True)  36.2 us
    all_to_all x1, blocking collectives, swap(): return lax.all_to_all(x, name, split_axis=0, concat_axis=0, tiled=True)  27.6 us
    ppermute x6, starting transfers between devices, grouped_velocity(): moved.append(lax.ppermute(velocity[level], both, route))  16.3 us
  transfers between devices with their start and end apart: 17, of which 13 were waited for; matrix products, arithmetic and copies ran while one was open for 1% of the time, Pallas kernels for 14%

profile of v2, /device:TPU:11, one launch (start us, length us, event | category | flops | bytes accessed | tf_op | source)
XLA Modules:
  0.0 580.4 jit_solution(15372462259106970087)
XLA Ops:
  7.6 27.6 %all_to_all.50 = f32[16,2,128,128]{3,2,1,0:T(8,128)} all-to-all(f32[16,2,128,128]{3,2,1,0:T(8,128)S(1)} %bitcast.15), channel_id=1, replica_groups=mesh['freq'=2,'slab'=16] {'freq'}, dimensions={0} | all-to-all | bytes 4194304 | tf_op jit(solution)/shard_map/all_to_all | solution.py:508
  35.2 7.5 %all-to-all-start.1 = ((f32[16,2,128,128]{3,2,1,0:T(8,128)}), f32[16,2,128,128]{3,2,1,0:T(8,128)S(1)}, u32[]{:S(2)}, u32[]{:S(2)}) async-start(f32[16,2,128,128]{3,2,1,0:T(8,128)} %all_to_all.50), calls=%async_computation.1 | async-start | bytes 4194304 | tf_op jit(solution)/shard_map/all_to_all | solution.py:508
  54.0 36.2 %all-to-all-done.1.got = f32[16,2,128,128]{3,2,1,0:T(8,128)S(1)} async-done(((f32[16,2,128,128]{3,2,1,0:T(8,128)}), f32[16,2,128,128]{3,2,1,0:T(8,128)S(1)}, u32[]{:S(2)}, u32[]{:S(2)}) %all-to-all-start.1) | async-done | bytes 2097184 | tf_op jit(solution)/shard_map/all_to_all | solution.py:508
  98.3 7.4 %shard_map.105 = f32[16,2,128,128]{3,2,1,0:T(8,128)} custom-call(f32[16,2,128,128]{3,2,1,0:T(8,128)} %shard_map.101.spec, f32[16,2,128,128]{3,2,1,0:T(8,128)} %get-tuple-element.19.shift, bf16[2,256,256]{2,1,0:T(8,128)(2,1)} %constant.65.clone.mat.mat_next, f32[16,2,128,128]{3,2,1,0:T(8,128)} %constant.68.clone.tw), custom_call_target="tpu_custom_call" | custom-call | flops 2800000000 | bytes 21000000 | tf_op jit(solution)/shard_map/pallas_call | solution.py:460
  105.7 14.5 %all-to-all-start.3 = ((f32[16,2,128,128]{3,2,1,0:T(8,128)}), f32[16,2,128,128]{3,2,1,0:T(8,128)S(1)}, u32[]{:S(2)}, u32[]{:S(2)}) async-start(f32[16,2,128,128]{3,2,1,0:T(8,128)} %shard_map.105), calls=%async_computation.3 | async-start | bytes 4194304 | tf_op jit(solution)/shard_map/back0_0/all_to_all | solution.py:511
  127.5 19.6 %all-to-all-done.3.got = f32[16,2,128,128]{3,2,1,0:T(8,128)S(1)} async-done(((f32[16,2,128,128]{3,2,1,0:T(8,128)}), f32[16,2,128,128]{3,2,1,0:T(8,128)S(1)}, u32[]{:S(2)}, u32[]{:S(2)}) %all-to-all-start.3) | async-done | bytes 2097184 | tf_op jit(solution)/shard_map/back0_0/all_to_all | solution.py:511
  162.0 16.3 %collective-permute-done.1.refs_0_ = f32[128,1024]{1,0:T(8,128)S(1)} collective-permute-done((f32[128,1024]{1,0:T(8,128)S(1)}, f32[128,1024]{1,0:T(8,128)S(1)}, u32[]{:S(2)}, u32[]{:S(2)}) %collective-permute-start.1) | collective-permute-done | bytes 524320 | tf_op jit(solution)/shard_map/vel0/ppermute | solution.py:533
  178.3 15.6 %collective-permute-done.2.refs_1_ = f32[128,1024]{1,0:T(8,128)S(1)} collective-permute-done((f32[128,1024]{1,0:T(8,128)S(1)}, f32[128,1024]{1,0:T(8,128)S(1)}, u32[]{:S(2)}, u32[]{:S(2)}) %collective-permute-start.2) | collective-permute-done | bytes 524320 | tf_op jit(solution)/shard_map/vel0/ppermute | solution.py:533
  207.6 10.0 %shard_map.107 = f32[16,2,128,128]{3,2,1,0:T(8,128)} custom-call(f32[16,2,128,128]{3,2,1,0:T(8,128)} %all-to-all-done.2.got, f32[2,128,2048]{2,1,0:T(8,128)} %get-tuple-element.18.weight, f32[2,128,2048]{2,1,0:T(8,128)} %shard_map.106.part, bf16[2,256,256]{2,1,0:T(8,128)(2,1)} %constant.67.clone.mat, f32[16,2,8,128]{3,2,1,0:T(8,128)} %constant.66.clone.tw, ...), custom_call_target="tpu_custom_call" | custom-call | flops 3600000000 | bytes 27000000 | tf_op jit(solution)/shard_map/pallas_call | solution.py:460
  217.6 10.7 %all-to-all-start.4 = ((f32[16,2,128,128]{3,2,1,0:T(8,128)}), f32[16,2,128,128]{3,2,1,0:T(8,128)S(1)}, u32[]{:S(2)}, u32[]{:S(2)}) async-start(f32[16,2,128,128]{3,2,1,0:T(8,128)} %shard_map.107), calls=%async_computation.4 | async-start | bytes 4194304 | tf_op jit(solution)/shard_map/all_to_all | solution.py:511
  236.9 18.4 %all-to-all-done.4.got = f32[16,2,128,128]{3,2,1,0:T(8,128)S(1)} async-done(((f32[16,2,128,128]{3,2,1,0:T(8,128)}), f32[16,2,128,128]{3,2,1,0:T(8,128)S(1)}, u32[]{:S(2)}, u32[]{:S(2)}) %all-to-all-start.4) | async-done | bytes 2097184 | tf_op jit(solution)/shard_map/all_to_all | solution.py:511
  263.3 7.4 %shard_map.112 = f32[16,2,128,128]{3,2,1,0:T(8,128)} custom-call(f32[16,2,128,128]{3,2,1,0:T(8,128)} %shard_map.108.spec, f32[16,2,128,128]{3,2,1,0:T(8,128)} %get-tuple-element.23.shift, bf16[2,256,256]{2,1,0:T(8,128)(2,1)} %constant.65.clone.mat.mat_next, f32[16,2,128,128]{3,2,1,0:T(8,128)} %constant.68.clone.tw), custom_call_target="tpu_custom_call" | custom-call | flops 2800000000 | bytes 21000000 | tf_op jit(solution)/shard_map/pallas_call | solution.py:460
  277.8 7.3 %shard_map.110 = f32[16,2,128,128]{3,2,1,0:T(8,128)} custom-call(f32[16,2,128,128]{3,2,1,0:T(8,128)} %shard_map.108.spec, f32[16,2,128,128]{3,2,1,0:T(8,128)} %get-tuple-element.21.shift, bf16[2,256,256]{2,1,0:T(8,128)(2,1)} %constant.65.clone.mat.mat_next, f32[16,2,128,128]{3,2,1,0:T(8,128)} %constant.68.clone.tw), custom_call_target="tpu_custom_call" | custom-call | flops 2800000000 | bytes 21000000 | tf_op jit(solution)/shard_map/pallas_call | solution.py:460
  285.1 19.6 %all-to-all-done.6.got = f32[16,2,128,128]{3,2,1,0:T(8,128)S(1)} async-done(((f32[16,2,128,128]{3,2,1,0:T(8,128)}), f32[16,2,128,128]{3,2,1,0:T(8,128)S(1)}, u32[]{:S(2)}, u32[]{:S(2)}) %all-to-all-start.6) | async-done | bytes 2097184 | tf_op jit(solution)/shard_map/back1_0/all_to_all | solution.py:511
  318.1 16.4 %collective-permute-done.3.refs_0_ = f32[128,1024]{1,0:T(8,128)S(1)} collective-permute-done((f32[128,1024]{1,0:T(8,128)S(1)}, f32[128,1024]{1,0:T(8,128)S(1)}, u32[]{:S(2)}, u32[]{:S(2)}) %collective-permute-start.3) | collective-permute-done | bytes 524320 | tf_op jit(solution)/shard_map/vel1/ppermute | solution.py:533
  334.5 16.8 %collective-permute-done.4.refs_1_ = f32[128,1024]{1,0:T(8,128)S(1)} collective-permute-done((f32[128,1024]{1,0:T(8,128)S(1)}, f32[128,1024]{1,0:T(8,128)S(1)}, u32[]{:S(2)}, u32[]{:S(2)}) %collective-permute-start.4) | collective-permute-done | bytes 524320 | tf_op jit(solution)/shard_map/vel1/ppermute | solution.py:533
  365.0 10.0 %shard_map.114 = f32[16,2,128,128]{3,2,1,0:T(8,128)} custom-call(f32[16,2,128,128]{3,2,1,0:T(8,128)} %all-to-all-done.5.got, f32[2,128,2048]{2,1,0:T(8,128)} %get-tuple-element.22.weight, f32[2,128,2048]{2,1,0:T(8,128)} %shard_map.113.part, bf16[2,256,256]{2,1,0:T(8,128)(2,1)} %constant.67.clone.mat, f32[16,2,8,128]{3,2,1,0:T(8,128)} %constant.66.clone.tw, ...), custom_call_target="tpu_custom_call" | custom-call | flops 3600000000 | bytes 27000000 | tf_op jit(solution)/shard_map/pallas_call | solution.py:460
  375.0 9.9 %all-to-all-start.7 = ((f32[16,2,128,128]{3,2,1,0:T(8,128)}), f32[16,2,128,128]{3,2,1,0:T(8,128)S(1)}, u32[]{:S(2)}, u32[]{:S(2)}) async-start(f32[16,2,128,128]{3,2,1,0:T(8,128)} %shard_map.114), calls=%async_computation.7 | async-start | bytes 4194304 | tf_op jit(solution)/shard_map/all_to_all | solution.py:511
  393.4 18.4 %all-to-all-done.7.got = f32[16,2,128,128]{3,2,1,0:T(8,128)S(1)} async-done(((f32[16,2,128,128]{3,2,1,0:T(8,128)}), f32[16,2,128,128]{3,2,1,0:T(8,128)S(1)}, u32[]{:S(2)}, u32[]{:S(2)}) %all-to-all-start.7) | async-done | bytes 2097184 | tf_op jit(solution)/shard_map/all_to_all | solution.py:511
  419.9 7.4 %shard_map.119 = f32[16,2,128,128]{3,2,1,0:T(8,128)} custom-call(f32[16,2,128,128]{3,2,1,0:T(8,128)} %shard_map.115.spec, f32[16,2,128,128]{3,2,1,0:T(8,128)} %get-tuple-element.27.shift, bf16[2,256,256]{2,1,0:T(8,128)(2,1)} %constant.65.clone.mat.mat_next, f32[16,2,128,128]{3,2,1,0:T(8,128)} %constant.68.clone.tw), custom_call_target="tpu_custom_call" | custom-call | flops 2800000000 | bytes 21000000 | tf_op jit(solution)/shard_map/pallas_call | solution.py:460
  441.7 19.6 %all-to-all-done.9.got = f32[16,2,128,128]{3,2,1,0:T(8,128)S(1)} async-done(((f32[16,2,128,128]{3,2,1,0:T(8,128)}), f32[16,2,128,128]{3,2,1,0:T(8,128)S(1)}, u32[]{:S(2)}, u32[]{:S(2)}) %all-to-all-start.9) | async-done | bytes 2097184 | tf_op jit(solution)/shard_map/back2_0/all_to_all | solution.py:511
  475.9 16.0 %collective-permute-done.5.refs_0_ = f32[128,1024]{1,0:T(8,128)S(1)} collective-permute-done((f32[128,1024]{1,0:T(8,128)S(1)}, f32[128,1024]{1,0:T(8,128)S(1)}, u32[]{:S(2)}, u32[]{:S(2)}) %collective-permute-start.5) | collective-permute-done | bytes 524320 | tf_op jit(solution)/shard_map/vel2/ppermute | solution.py:533
  491.9 16.9 %collective-permute-done.6.refs_1_ = f32[128,1024]{1,0:T(8,128)S(1)} collective-permute-done((f32[128,1024]{1,0:T(8,128)S(1)}, f32[128,1024]{1,0:T(8,128)S(1)}, u32[]{:S(2)}, u32[]{:S(2)}) %collective-permute-start.6) | collective-permute-done | bytes 524320 | tf_op jit(solution)/shard_map/vel2/ppermute | solution.py:533
  534.8 44.3 %collective-permute-done.7 = f32[2,128,2048]{2,1,0:T(8,128)S(1)} collective-permute-done((f32[2,128,2048]{2,1,0:T(8,128)}, f32[2,128,2048]{2,1,0:T(8,128)S(1)}, u32[]{:S(2)}, u32[]{:S(2)}) %collective-permute-start.7) | collective-permute-done | bytes 2097184 | tf_op jit(solution)/shard_map/ppermute | solution.py:565
  (68 shorter events, 186.3 us)
Async XLA Ops:
  35.2 9.4 %copy-start.6 = (f32[3,2]{0,1:T(2,128)S(1)}, f32[3,2]{0,1:T(2,128)}, u32[]{:S(2)}) copy-start(f32[3,2]{0,1:T(2,128)} %param.13) | copy-start | bytes 76
  35.2 54.9 %all-to-all-start.1 = ((f32[16,2,128,128]{3,2,1,0:T(8,128)}), f32[16,2,128,128]{3,2,1,0:T(8,128)S(1)}, u32[]{:S(2)}, u32[]{:S(2)}) async-start(f32[16,2,128,128]{3,2,1,0:T(8,128)} %all_to_all.50), calls=%async_computation.1 | async-start | bytes 4194304 | tf_op jit(solution)/shard_map/all_to_all | solution.py:508
  42.8 2.1 collective-permute-start
  105.7 41.4 %all-to-all-start.3 = ((f32[16,2,128,128]{3,2,1,0:T(8,128)}), f32[16,2,128,128]{3,2,1,0:T(8,128)S(1)}, u32[]{:S(2)}, u32[]{:S(2)}) async-start(f32[16,2,128,128]{3,2,1,0:T(8,128)} %shard_map.105), calls=%async_computation.3 | async-start | bytes 4194304 | tf_op jit(solution)/shard_map/back0_0/all_to_all | solution.py:511
  147.1 1.3 copy-start
  148.5 59.1 %all-to-all-start.2 = ((f32[16,2,128,128]{3,2,1,0:T(8,128)}), f32[16,2,128,128]{3,2,1,0:T(8,128)}, u32[]{:S(2)}, u32[]{:S(2)}) async-start(f32[16,2,128,128]{3,2,1,0:T(8,128)} %shard_map.103), calls=%async_computation.2 | async-start | bytes 4194304 | tf_op jit(solution)/shard_map/back0_1/all_to_all | solution.py:511
  156.9 21.4 %collective-permute-start.1 = (f32[128,1024]{1,0:T(8,128)S(1)}, f32[128,1024]{1,0:T(8,128)S(1)}, u32[]{:S(2)}, u32[]{:S(2)}) collective-permute-start(f32[128,1024]{1,0:T(8,128)S(1)} %get-tuple-element.33), channel_id=1, source_target_pairs={{0,0},{1,1},{2,2},{3,3},{4,24},{5,25},{6,26},{7,27},{8,4},{9,5},{1... | collective-permute-start | bytes 1572872 | tf_op jit(solution)/shard_map/vel0/ppermute | solution.py:533
  158.9 35.0 %collective-permute-start.2 = (f32[128,1024]{1,0:T(8,128)S(1)}, f32[128,1024]{1,0:T(8,128)S(1)}, u32[]{:S(2)}, u32[]{:S(2)}) collective-permute-start(f32[128,1024]{1,0:T(8,128)S(1)} %get-tuple-element.33), channel_id=1, source_target_pairs={{0,8},{1,9},{2,10},{3,11},{4,16},{5,17},{6,18},{7,19},{8,12},{9,13... | collective-permute-start | bytes 1572872 | tf_op jit(solution)/shard_map/vel0/ppermute | solution.py:533
  178.3 15.6 %copy-start.7 = (f32[128,1024]{1,0:T(8,128)}, f32[128,1024]{1,0:T(8,128)S(1)}, u32[]{:S(2)}) copy-start(f32[128,1024]{1,0:T(8,128)S(1)} %collective-permute-done.1.refs_0_) | copy-start | bytes 1572868
  217.6 37.7 %all-to-all-start.4 = ((f32[16,2,128,128]{3,2,1,0:T(8,128)}), f32[16,2,128,128]{3,2,1,0:T(8,128)S(1)}, u32[]{:S(2)}, u32[]{:S(2)}) async-start(f32[16,2,128,128]{3,2,1,0:T(8,128)} %shard_map.107), calls=%async_computation.4 | async-start | bytes 4194304 | tf_op jit(solution)/shard_map/all_to_all | solution.py:511
  270.7 34.0 %all-to-all-start.6 = ((f32[16,2,128,128]{3,2,1,0:T(8,128)}), f32[16,2,128,128]{3,2,1,0:T(8,128)S(1)}, u32[]{:S(2)}, u32[]{:S(2)}) async-start(f32[16,2,128,128]{3,2,1,0:T(8,128)} %shard_map.112), calls=%async_computation.6 | async-start | bytes 4194304 | tf_op jit(solution)/shard_map/back1_0/all_to_all | solution.py:511
  304.7 1.3 copy-start.3
  306.0 58.9 %all-to-all-start.5 = ((f32[16,2,128,128]{3,2,1,0:T(8,128)}), f32[16,2,128,128]{3,2,1,0:T(8,128)}, u32[]{:S(2)}, u32[]{:S(2)}) async-start(f32[16,2,128,128]{3,2,1,0:T(8,128)} %shard_map.110), calls=%async_computation.5 | async-start | bytes 4194304 | tf_op jit(solution)/shard_map/back1_1/all_to_all | solution.py:511
  313.1 21.5 %collective-permute-start.3 = (f32[128,1024]{1,0:T(8,128)S(1)}, f32[128,1024]{1,0:T(8,128)S(1)}, u32[]{:S(2)}, u32[]{:S(2)}) collective-permute-start(f32[128,1024]{1,0:T(8,128)S(1)} %get-tuple-element.34), channel_id=1, source_target_pairs={{0,0},{1,1},{2,2},{3,3},{4,24},{5,25},{6,26},{7,27},{8,4},{9,5},{1... | collective-permute-start | bytes 1572872 | tf_op jit(solution)/shard_map/vel1/ppermute | solution.py:533
  315.0 36.3 %collective-permute-start.4 = (f32[128,1024]{1,0:T(8,128)S(1)}, f32[128,1024]{1,0:T(8,128)S(1)}, u32[]{:S(2)}, u32[]{:S(2)}) collective-permute-start(f32[128,1024]{1,0:T(8,128)S(1)} %get-tuple-element.34), channel_id=1, source_target_pairs={{0,8},{1,9},{2,10},{3,11},{4,16},{5,17},{6,18},{7,19},{8,12},{9,13... | collective-permute-start | bytes 1572872 | tf_op jit(solution)/shard_map/vel1/ppermute | solution.py:533
  334.5 16.8 %copy-start.10 = (f32[128,1024]{1,0:T(8,128)}, f32[128,1024]{1,0:T(8,128)S(1)}, u32[]{:S(2)}) copy-start(f32[128,1024]{1,0:T(8,128)S(1)} %collective-permute-done.3.refs_0_) | copy-start | bytes 1572868
  375.0 36.9 %all-to-all-start.7 = ((f32[16,2,128,128]{3,2,1,0:T(8,128)}), f32[16,2,128,128]{3,2,1,0:T(8,128)S(1)}, u32[]{:S(2)}, u32[]{:S(2)}) async-start(f32[16,2,128,128]{3,2,1,0:T(8,128)} %shard_map.114), calls=%async_computation.7 | async-start | bytes 4194304 | tf_op jit(solution)/shard_map/all_to_all | solution.py:511
  427.3 34.0 %all-to-all-start.9 = ((f32[16,2,128,128]{3,2,1,0:T(8,128)}), f32[16,2,128,128]{3,2,1,0:T(8,128)S(1)}, u32[]{:S(2)}, u32[]{:S(2)}) async-start(f32[16,2,128,128]{3,2,1,0:T(8,128)} %shard_map.119), calls=%async_computation.9 | async-start | bytes 4194304 | tf_op jit(solution)/shard_map/back2_0/all_to_all | solution.py:511
  461.3 1.3 copy-start.2
  462.6 59.8 %all-to-all-start.8 = ((f32[16,2,128,128]{3,2,1,0:T(8,128)}), f32[16,2,128,128]{3,2,1,0:T(8,128)}, u32[]{:S(2)}, u32[]{:S(2)}) async-start(f32[16,2,128,128]{3,2,1,0:T(8,128)} %shard_map.117), calls=%async_computation.8 | async-start | bytes 4194304 | tf_op jit(solution)/shard_map/back2_1/all_to_all | solution.py:511
  469.6 22.3 %collective-permute-start.5 = (f32[128,1024]{1,0:T(8,128)S(1)}, f32[128,1024]{1,0:T(8,128)S(1)}, u32[]{:S(2)}, u32[]{:S(2)}) collective-permute-start(f32[128,1024]{1,0:T(8,128)S(1)} %get-tuple-element.32), channel_id=1, source_target_pairs={{0,0},{1,1},{2,2},{3,3},{4,24},{5,25},{6,26},{7,27},{8,4},{9,5},{1... | collective-permute-start | bytes 1572872 | tf_op jit(solution)/shard_map/vel2/ppermute | solution.py:533
  472.8 35.9 %collective-permute-start.6 = (f32[128,1024]{1,0:T(8,128)S(1)}, f32[128,1024]{1,0:T(8,128)S(1)}, u32[]{:S(2)}, u32[]{:S(2)}) collective-permute-start(f32[128,1024]{1,0:T(8,128)S(1)} %get-tuple-element.32), channel_id=1, source_target_pairs={{0,8},{1,9},{2,10},{3,11},{4,16},{5,17},{6,18},{7,19},{8,12},{9,13... | collective-permute-start | bytes 1572872 | tf_op jit(solution)/shard_map/vel2/ppermute | solution.py:533
  491.9 16.9 %copy-start.9 = (f32[128,1024]{1,0:T(8,128)}, f32[128,1024]{1,0:T(8,128)S(1)}, u32[]{:S(2)}) copy-start(f32[128,1024]{1,0:T(8,128)S(1)} %collective-permute-done.5.refs_0_) | copy-start | bytes 1572868
  529.7 49.4 %collective-permute-start.7 = (f32[2,128,2048]{2,1,0:T(8,128)}, f32[2,128,2048]{2,1,0:T(8,128)S(1)}, u32[]{:S(2)}, u32[]{:S(2)}) collective-permute-start(f32[2,128,2048]{2,1,0:T(8,128)} %shard_map.121), channel_id=1, source_target_pairs={{0,0},{1,1},{2,2},{3,3},{16,4},{17,5},{18,6},{19,7},{4,8},{5,9},{6... | collective-permute-start | bytes 6291464 | tf_op jit(solution)/shard_map/ppermute | solution.py:565
  (6 other events, 6.3 us)

commit v3 on v2

--- a/solution.py
+++ b/solution.py
@@ -523,14 +523,14 @@
     sends = sends.swapaxes(0, 1).reshape(across)
     got = swap(swap(sends, "freq"), "slab")
 
-    def grouped_velocity(level):
+    def grouped_velocity(values):
         moved = []
         for shift in range(freq_count):
             route = []
             for y, s in everyone:
                 to_row, place = owner(s)
                 route.append((y * slabs + s, device(to_row, (to_row + y + shift) % freq_count, place)))
-            moved.append(lax.ppermute(velocity[level], both, route))
+            moved.append(lax.ppermute(values, both, route))
         return moved
 
     order = ((slab_index // group + freq_count - row) % freq_count).astype(jnp.int32)[None]
@@ -539,8 +539,9 @@
         last = level == depth - 1
         if level:
             got = exchange(part_send)
-        with jax.named_scope(f"vel{level}"):
-            tiles = grouped_velocity(level)
+        else:
+            got, velocity = lax.optimization_barrier((got, velocity))
+        tiles = grouped_velocity(velocity[level])
         scal = jnp.concatenate([group_freq, ref_slow[level]])
         shift = call(
             functools.partial(spread_kernel, slabs, width_x), across, None, 8, scal, fy2, scalars=1, outputs=2
@@ -550,8 +551,7 @@
         back = []
         for branch in range(2):
             sent = call(column_back_kernel, across, across, 7, spec, shift[branch], col_inv, col_tw)
-            with jax.named_scope(f"back{level}_{branch}"):
-                back.append(exchange(sent))
+            back.append(exchange(sent))
         part = call(row_back_kernel, (2, rows, width_y), row_work, 6, back[0], weight[0], row_inv, row_tw)
         part_send = call(
             functools.partial(row_join_kernel, last),
@@ -576,12 +576,13 @@
             and wavefield.shape[1] == mesh.shape["freq"] == 2
             and slabs % 4 == 0
         )
-        return jax.shard_map(
+        step = jax.shard_map(
             shards if whole_tiles else shards_generic,
             mesh=mesh,
             in_specs=(P(None, "freq", "slab", None), P("freq"), P(None, "slab", "freq"), P()),
             out_specs=P(None, "freq", "slab", None),
             check_vma=False,
-        )(wavefield, freqs, velocity, ref_slow)
+        )
+        return step(wavefield, freqs, velocity, ref_slow)
 
     return program

time: 586 us -> 586 us (level)
  no operation moved by 1% of the time
where the time goes in v3:
time: 586 us; the launch traced here: 580 us
  waiting for transfers between devices  274 us (47%)
  Pallas kernels  158 us (27%)
  starting transfers between devices  101 us (17%)
  blocking collectives  27.6 us (5%)
  local copies, waits for them, and re-layouts  15.6 us (3%)
    pallas_call x22, Pallas kernels, call(): pl.pallas_call(body, out_shape=result if outputs == 1 else (result,) * ou...  158 us
    ppermute x6, waiting for transfers between devices, grouped_velocity(): moved.append(lax.ppermute(values, both, route))  97.9 us
    all_to_all x8, waiting for transfers between devices, exchange(): lax.all_to_all(x, both, split_axis=0, concat_axis=0, tiled=True, axis_ind...  95.6 us
    all_to_all x8, starting transfers between devices, exchange(): lax.all_to_all(x, both, split_axis=0, concat_axis=0, tiled=True, axis_ind...  70.3 us
    ppermute x1, waiting for transfers between devices, shards(): return lax.ppermute(part_send, both, leave)[:, None]  44.3 us
    all_to_all x1, waiting for transfers between devices, swap(): return lax.all_to_all(x, name, split_axis=0, concat_axis=0, tiled=True)  36.2 us
    all_to_all x1, blocking collectives, swap(): return lax.all_to_all(x, name, split_axis=0, concat_axis=0, tiled=True)  27.6 us
    ppermute x6, starting transfers between devices, grouped_velocity(): moved.append(lax.ppermute(values, both, route))  16.3 us
  transfers between devices with their start and end apart: 17, of which 13 were waited for; matrix products, arithmetic and copies ran while one was open for 1% of the time, Pallas kernels for 14%

profile of v3, /device:TPU:11, one launch (start us, length us, event | category | flops | bytes accessed | tf_op | source)
XLA Modules:
  0.0 580.4 jit_solution(7261002879204940277)
XLA Ops:
  7.6 27.6 %all_to_all.50 = f32[16,2,128,128]{3,2,1,0:T(8,128)} all-to-all(f32[16,2,128,128]{3,2,1,0:T(8,128)S(1)} %bitcast.15), channel_id=1, replica_groups=mesh['freq'=2,'slab'=16] {'freq'}, dimensions={0} | all-to-all | bytes 4194304 | tf_op jit(solution)/shard_map/all_to_all | solution.py:508
  35.2 7.5 %all-to-all-start.1 = ((f32[16,2,128,128]{3,2,1,0:T(8,128)}), f32[16,2,128,128]{3,2,1,0:T(8,128)S(1)}, u32[]{:S(2)}, u32[]{:S(2)}) async-start(f32[16,2,128,128]{3,2,1,0:T(8,128)} %all_to_all.50), calls=%async_computation.1 | async-start | bytes 4194304 | tf_op jit(solution)/shard_map/all_to_all | solution.py:508
  54.0 36.2 %all-to-all-done.1.got = f32[16,2,128,128]{3,2,1,0:T(8,128)S(1)} async-done(((f32[16,2,128,128]{3,2,1,0:T(8,128)}), f32[16,2,128,128]{3,2,1,0:T(8,128)S(1)}, u32[]{:S(2)}, u32[]{:S(2)}) %all-to-all-start.1) | async-done | bytes 2097184 | tf_op jit(solution)/shard_map/all_to_all | solution.py:508
  98.3 7.4 %shard_map.105 = f32[16,2,128,128]{3,2,1,0:T(8,128)} custom-call(f32[16,2,128,128]{3,2,1,0:T(8,128)} %shard_map.101.spec, f32[16,2,128,128]{3,2,1,0:T(8,128)} %get-tuple-element.23.shift, bf16[2,256,256]{2,1,0:T(8,128)(2,1)} %constant.65.clone.mat.mat_next, f32[16,2,128,128]{3,2,1,0:T(8,128)} %constant.68.clone.tw), custom_call_target="tpu_custom_call" | custom-call | flops 2800000000 | bytes 21000000 | tf_op jit(solution)/shard_map/pallas_call | solution.py:460
  105.7 14.5 %all-to-all-start.3 = ((f32[16,2,128,128]{3,2,1,0:T(8,128)}), f32[16,2,128,128]{3,2,1,0:T(8,128)S(1)}, u32[]{:S(2)}, u32[]{:S(2)}) async-start(f32[16,2,128,128]{3,2,1,0:T(8,128)} %shard_map.105), calls=%async_computation.3 | async-start | bytes 4194304 | tf_op jit(solution)/shard_map/all_to_all | solution.py:511
  127.5 19.6 %all-to-all-done.3.got = f32[16,2,128,128]{3,2,1,0:T(8,128)S(1)} async-done(((f32[16,2,128,128]{3,2,1,0:T(8,128)}), f32[16,2,128,128]{3,2,1,0:T(8,128)S(1)}, u32[]{:S(2)}, u32[]{:S(2)}) %all-to-all-start.3) | async-done | bytes 2097184 | tf_op jit(solution)/shard_map/all_to_all | solution.py:511
  162.0 16.3 %collective-permute-done.1.refs_0_ = f32[128,1024]{1,0:T(8,128)S(1)} collective-permute-done((f32[128,1024]{1,0:T(8,128)S(1)}, f32[128,1024]{1,0:T(8,128)S(1)}, u32[]{:S(2)}, u32[]{:S(2)}) %collective-permute-start.1) | collective-permute-done | bytes 524320 | tf_op jit(solution)/shard_map/ppermute | solution.py:533
  178.3 15.6 %collective-permute-done.2.refs_1_ = f32[128,1024]{1,0:T(8,128)S(1)} collective-permute-done((f32[128,1024]{1,0:T(8,128)S(1)}, f32[128,1024]{1,0:T(8,128)S(1)}, u32[]{:S(2)}, u32[]{:S(2)}) %collective-permute-start.2) | collective-permute-done | bytes 524320 | tf_op jit(solution)/shard_map/ppermute | solution.py:533
  207.6 10.0 %shard_map.107 = f32[16,2,128,128]{3,2,1,0:T(8,128)} custom-call(f32[16,2,128,128]{3,2,1,0:T(8,128)} %all-to-all-done.2.got, f32[2,128,2048]{2,1,0:T(8,128)} %get-tuple-element.22.weight, f32[2,128,2048]{2,1,0:T(8,128)} %shard_map.106.part, bf16[2,256,256]{2,1,0:T(8,128)(2,1)} %constant.67.clone.mat, f32[16,2,8,128]{3,2,1,0:T(8,128)} %constant.66.clone.tw, ...), custom_call_target="tpu_custom_call" | custom-call | flops 3600000000 | bytes 27000000 | tf_op jit(solution)/shard_map/pallas_call | solution.py:460
  217.6 10.7 %all-to-all-start.4 = ((f32[16,2,128,128]{3,2,1,0:T(8,128)}), f32[16,2,128,128]{3,2,1,0:T(8,128)S(1)}, u32[]{:S(2)}, u32[]{:S(2)}) async-start(f32[16,2,128,128]{3,2,1,0:T(8,128)} %shard_map.107), calls=%async_computation.4 | async-start | bytes 4194304 | tf_op jit(solution)/shard_map/all_to_all | solution.py:511
  236.9 18.4 %all-to-all-done.4.got = f32[16,2,128,128]{3,2,1,0:T(8,128)S(1)} async-done(((f32[16,2,128,128]{3,2,1,0:T(8,128)}), f32[16,2,128,128]{3,2,1,0:T(8,128)S(1)}, u32[]{:S(2)}, u32[]{:S(2)}) %all-to-all-start.4) | async-done | bytes 2097184 | tf_op jit(solution)/shard_map/all_to_all | solution.py:511
  263.3 7.4 %shard_map.112 = f32[16,2,128,128]{3,2,1,0:T(8,128)} custom-call(f32[16,2,128,128]{3,2,1,0:T(8,128)} %shard_map.108.spec, f32[16,2,128,128]{3,2,1,0:T(8,128)} %get-tuple-element.27.shift, bf16[2,256,256]{2,1,0:T(8,128)(2,1)} %constant.65.clone.mat.mat_next, f32[16,2,128,128]{3,2,1,0:T(8,128)} %constant.68.clone.tw), custom_call_target="tpu_custom_call" | custom-call | flops 2800000000 | bytes 21000000 | tf_op jit(solution)/shard_map/pallas_call | solution.py:460
  277.8 7.3 %shard_map.110 = f32[16,2,128,128]{3,2,1,0:T(8,128)} custom-call(f32[16,2,128,128]{3,2,1,0:T(8,128)} %shard_map.108.spec, f32[16,2,128,128]{3,2,1,0:T(8,128)} %get-tuple-element.25.shift, bf16[2,256,256]{2,1,0:T(8,128)(2,1)} %constant.65.clone.mat.mat_next, f32[16,2,128,128]{3,2,1,0:T(8,128)} %constant.68.clone.tw), custom_call_target="tpu_custom_call" | custom-call | flops 2800000000 | bytes 21000000 | tf_op jit(solution)/shard_map/pallas_call | solution.py:460
  285.1 19.6 %all-to-all-done.6.got = f32[16,2,128,128]{3,2,1,0:T(8,128)S(1)} async-done(((f32[16,2,128,128]{3,2,1,0:T(8,128)}), f32[16,2,128,128]{3,2,1,0:T(8,128)S(1)}, u32[]{:S(2)}, u32[]{:S(2)}) %all-to-all-start.6) | async-done | bytes 2097184 | tf_op jit(solution)/shard_map/all_to_all | solution.py:511
  318.1 16.4 %collective-permute-done.3.refs_0_ = f32[128,1024]{1,0:T(8,128)S(1)} collective-permute-done((f32[128,1024]{1,0:T(8,128)S(1)}, f32[128,1024]{1,0:T(8,128)S(1)}, u32[]{:S(2)}, u32[]{:S(2)}) %collective-permute-start.3) | collective-permute-done | bytes 524320 | tf_op jit(solution)/shard_map/ppermute | solution.py:533
  334.5 16.8 %collective-permute-done.4.refs_1_ = f32[128,1024]{1,0:T(8,128)S(1)} collective-permute-done((f32[128,1024]{1,0:T(8,128)S(1)}, f32[128,1024]{1,0:T(8,128)S(1)}, u32[]{:S(2)}, u32[]{:S(2)}) %collective-permute-start.4) | collective-permute-done | bytes 524320 | tf_op jit(solution)/shard_map/ppermute | solution.py:533
  365.0 10.0 %shard_map.114 = f32[16,2,128,128]{3,2,1,0:T(8,128)} custom-call(f32[16,2,128,128]{3,2,1,0:T(8,128)} %all-to-all-done.5.got, f32[2,128,2048]{2,1,0:T(8,128)} %get-tuple-element.26.weight, f32[2,128,2048]{2,1,0:T(8,128)} %shard_map.113.part, bf16[2,256,256]{2,1,0:T(8,128)(2,1)} %constant.67.clone.mat, f32[16,2,8,128]{3,2,1,0:T(8,128)} %constant.66.clone.tw, ...), custom_call_target="tpu_custom_call" | custom-call | flops 3600000000 | bytes 27000000 | tf_op jit(solution)/shard_map/pallas_call | solution.py:460
  375.0 9.9 %all-to-all-start.7 = ((f32[16,2,128,128]{3,2,1,0:T(8,128)}), f32[16,2,128,128]{3,2,1,0:T(8,128)S(1)}, u32[]{:S(2)}, u32[]{:S(2)}) async-start(f32[16,2,128,128]{3,2,1,0:T(8,128)} %shard_map.114), calls=%async_computation.7 | async-start | bytes 4194304 | tf_op jit(solution)/shard_map/all_to_all | solution.py:511
  393.4 18.4 %all-to-all-done.7.got = f32[16,2,128,128]{3,2,1,0:T(8,128)S(1)} async-done(((f32[16,2,128,128]{3,2,1,0:T(8,128)}), f32[16,2,128,128]{3,2,1,0:T(8,128)S(1)}, u32[]{:S(2)}, u32[]{:S(2)}) %all-to-all-start.7) | async-done | bytes 2097184 | tf_op jit(solution)/shard_map/all_to_all | solution.py:511
  419.9 7.4 %shard_map.119 = f32[16,2,128,128]{3,2,1,0:T(8,128)} custom-call(f32[16,2,128,128]{3,2,1,0:T(8,128)} %shard_map.115.spec, f32[16,2,128,128]{3,2,1,0:T(8,128)} %get-tuple-element.31.shift, bf16[2,256,256]{2,1,0:T(8,128)(2,1)} %constant.65.clone.mat.mat_next, f32[16,2,128,128]{3,2,1,0:T(8,128)} %constant.68.clone.tw), custom_call_target="tpu_custom_call" | custom-call | flops 2800000000 | bytes 21000000 | tf_op jit(solution)/shard_map/pallas_call | solution.py:460
  441.7 19.6 %all-to-all-done.9.got = f32[16,2,128,128]{3,2,1,0:T(8,128)S(1)} async-done(((f32[16,2,128,128]{3,2,1,0:T(8,128)}), f32[16,2,128,128]{3,2,1,0:T(8,128)S(1)}, u32[]{:S(2)}, u32[]{:S(2)}) %all-to-all-start.9) | async-done | bytes 2097184 | tf_op jit(solution)/shard_map/all_to_all | solution.py:511
  475.9 16.0 %collective-permute-done.5.refs_0_ = f32[128,1024]{1,0:T(8,128)S(1)} collective-permute-done((f32[128,1024]{1,0:T(8,128)S(1)}, f32[128,1024]{1,0:T(8,128)S(1)}, u32[]{:S(2)}, u32[]{:S(2)}) %collective-permute-start.5) | collective-permute-done | bytes 524320 | tf_op jit(solution)/shard_map/ppermute | solution.py:533
  491.9 16.9 %collective-permute-done.6.refs_1_ = f32[128,1024]{1,0:T(8,128)S(1)} collective-permute-done((f32[128,1024]{1,0:T(8,128)S(1)}, f32[128,1024]{1,0:T(8,128)S(1)}, u32[]{:S(2)}, u32[]{:S(2)}) %collective-permute-start.6) | collective-permute-done | bytes 524320 | tf_op jit(solution)/shard_map/ppermute | solution.py:533
  534.8 44.3 %collective-permute-done.7 = f32[2,128,2048]{2,1,0:T(8,128)S(1)} collective-permute-done((f32[2,128,2048]{2,1,0:T(8,128)}, f32[2,128,2048]{2,1,0:T(8,128)S(1)}, u32[]{:S(2)}, u32[]{:S(2)}) %collective-permute-start.7) | collective-permute-done | bytes 2097184 | tf_op jit(solution)/shard_map/ppermute | solution.py:565
  (68 shorter events, 186.3 us)
Async XLA Ops:
  35.2 9.4 %copy-start.6 = (f32[3,2]{0,1:T(2,128)S(1)}, f32[3,2]{0,1:T(2,128)}, u32[]{:S(2)}) copy-start(f32[3,2]{0,1:T(2,128)} %param.13) | copy-start | bytes 76
  35.2 54.9 %all-to-all-start.1 = ((f32[16,2,128,128]{3,2,1,0:T(8,128)}), f32[16,2,128,128]{3,2,1,0:T(8,128)S(1)}, u32[]{:S(2)}, u32[]{:S(2)}) async-start(f32[16,2,128,128]{3,2,1,0:T(8,128)} %all_to_all.50), calls=%async_computation.1 | async-start | bytes 4194304 | tf_op jit(solution)/shard_map/all_to_all | solution.py:508
  42.8 2.1 collective-permute-start
  105.7 41.4 %all-to-all-start.3 = ((f32[16,2,128,128]{3,2,1,0:T(8,128)}), f32[16,2,128,128]{3,2,1,0:T(8,128)S(1)}, u32[]{:S(2)}, u32[]{:S(2)}) async-start(f32[16,2,128,128]{3,2,1,0:T(8,128)} %shard_map.105), calls=%async_computation.3 | async-start | bytes 4194304 | tf_op jit(solution)/shard_map/all_to_all | solution.py:511
  147.1 1.3 copy-start
  148.5 59.1 %all-to-all-start.2 = ((f32[16,2,128,128]{3,2,1,0:T(8,128)}), f32[16,2,128,128]{3,2,1,0:T(8,128)}, u32[]{:S(2)}, u32[]{:S(2)}) async-start(f32[16,2,128,128]{3,2,1,0:T(8,128)} %shard_map.103), calls=%async_computation.2 | async-start | bytes 4194304 | tf_op jit(solution)/shard_map/all_to_all | solution.py:511
  156.9 21.4 %collective-permute-start.1 = (f32[128,1024]{1,0:T(8,128)S(1)}, f32[128,1024]{1,0:T(8,128)S(1)}, u32[]{:S(2)}, u32[]{:S(2)}) collective-permute-start(f32[128,1024]{1,0:T(8,128)S(1)} %get-tuple-element.38), channel_id=1, source_target_pairs={{0,0},{1,1},{2,2},{3,3},{4,24},{5,25},{6,26},{7,27},{8,4},{9,5},{1... | collective-permute-start | bytes 1572872 | tf_op jit(solution)/shard_map/ppermute | solution.py:533
  158.9 35.0 %collective-permute-start.2 = (f32[128,1024]{1,0:T(8,128)S(1)}, f32[128,1024]{1,0:T(8,128)S(1)}, u32[]{:S(2)}, u32[]{:S(2)}) collective-permute-start(f32[128,1024]{1,0:T(8,128)S(1)} %get-tuple-element.38), channel_id=1, source_target_pairs={{0,8},{1,9},{2,10},{3,11},{4,16},{5,17},{6,18},{7,19},{8,12},{9,13... | collective-permute-start | bytes 1572872 | tf_op jit(solution)/shard_map/ppermute | solution.py:533
  178.3 15.6 %copy-start.7 = (f32[128,1024]{1,0:T(8,128)}, f32[128,1024]{1,0:T(8,128)S(1)}, u32[]{:S(2)}) copy-start(f32[128,1024]{1,0:T(8,128)S(1)} %collective-permute-done.1.refs_0_) | copy-start | bytes 1572868
  217.6 37.7 %all-to-all-start.4 = ((f32[16,2,128,128]{3,2,1,0:T(8,128)}), f32[16,2,128,128]{3,2,1,0:T(8,128)S(1)}, u32[]{:S(2)}, u32[]{:S(2)}) async-start(f32[16,2,128,128]{3,2,1,0:T(8,128)} %shard_map.107), calls=%async_computation.4 | async-start | bytes 4194304 | tf_op jit(solution)/shard_map/all_to_all | solution.py:511
  270.7 34.0 %all-to-all-start.6 = ((f32[16,2,128,128]{3,2,1,0:T(8,128)}), f32[16,2,128,128]{3,2,1,0:T(8,128)S(1)}, u32[]{:S(2)}, u32[]{:S(2)}) async-start(f32[16,2,128,128]{3,2,1,0:T(8,128)} %shard_map.112), calls=%async_computation.6 | async-start | bytes 4194304 | tf_op jit(solution)/shard_map/all_to_all | solution.py:511
  304.7 1.3 copy-start.3
  306.0 58.9 %all-to-all-start.5 = ((f32[16,2,128,128]{3,2,1,0:T(8,128)}), f32[16,2,128,128]{3,2,1,0:T(8,128)}, u32[]{:S(2)}, u32[]{:S(2)}) async-start(f32[16,2,128,128]{3,2,1,0:T(8,128)} %shard_map.110), calls=%async_computation.5 | async-start | bytes 4194304 | tf_op jit(solution)/shard_map/all_to_all | solution.py:511
  313.1 21.5 %collective-permute-start.3 = (f32[128,1024]{1,0:T(8,128)S(1)}, f32[128,1024]{1,0:T(8,128)S(1)}, u32[]{:S(2)}, u32[]{:S(2)}) collective-permute-start(f32[128,1024]{1,0:T(8,128)S(1)} %get-tuple-element.37), channel_id=1, source_target_pairs={{0,0},{1,1},{2,2},{3,3},{4,24},{5,25},{6,26},{7,27},{8,4},{9,5},{1... | collective-permute-start | bytes 1572872 | tf_op jit(solution)/shard_map/ppermute | solution.py:533
  315.0 36.3 %collective-permute-start.4 = (f32[128,1024]{1,0:T(8,128)S(1)}, f32[128,1024]{1,0:T(8,128)S(1)}, u32[]{:S(2)}, u32[]{:S(2)}) collective-permute-start(f32[128,1024]{1,0:T(8,128)S(1)} %get-tuple-element.37), channel_id=1, source_target_pairs={{0,8},{1,9},{2,10},{3,11},{4,16},{5,17},{6,18},{7,19},{8,12},{9,13... | collective-permute-start | bytes 1572872 | tf_op jit(solution)/shard_map/ppermute | solution.py:533
  334.5 16.8 %copy-start.10 = (f32[128,1024]{1,0:T(8,128)}, f32[128,1024]{1,0:T(8,128)S(1)}, u32[]{:S(2)}) copy-start(f32[128,1024]{1,0:T(8,128)S(1)} %collective-permute-done.3.refs_0_) | copy-start | bytes 1572868
  375.0 36.9 %all-to-all-start.7 = ((f32[16,2,128,128]{3,2,1,0:T(8,128)}), f32[16,2,128,128]{3,2,1,0:T(8,128)S(1)}, u32[]{:S(2)}, u32[]{:S(2)}) async-start(f32[16,2,128,128]{3,2,1,0:T(8,128)} %shard_map.114), calls=%async_computation.7 | async-start | bytes 4194304 | tf_op jit(solution)/shard_map/all_to_all | solution.py:511
  427.3 34.0 %all-to-all-start.9 = ((f32[16,2,128,128]{3,2,1,0:T(8,128)}), f32[16,2,128,128]{3,2,1,0:T(8,128)S(1)}, u32[]{:S(2)}, u32[]{:S(2)}) async-start(f32[16,2,128,128]{3,2,1,0:T(8,128)} %shard_map.119), calls=%async_computation.9 | async-start | bytes 4194304 | tf_op jit(solution)/shard_map/all_to_all | solution.py:511
  461.3 1.3 copy-start.2
  462.6 59.8 %all-to-all-start.8 = ((f32[16,2,128,128]{3,2,1,0:T(8,128)}), f32[16,2,128,128]{3,2,1,0:T(8,128)}, u32[]{:S(2)}, u32[]{:S(2)}) async-start(f32[16,2,128,128]{3,2,1,0:T(8,128)} %shard_map.117), calls=%async_computation.8 | async-start | bytes 4194304 | tf_op jit(solution)/shard_map/all_to_all | solution.py:511
  469.6 22.3 %collective-permute-start.5 = (f32[128,1024]{1,0:T(8,128)S(1)}, f32[128,1024]{1,0:T(8,128)S(1)}, u32[]{:S(2)}, u32[]{:S(2)}) collective-permute-start(f32[128,1024]{1,0:T(8,128)S(1)} %get-tuple-element.36), channel_id=1, source_target_pairs={{0,0},{1,1},{2,2},{3,3},{4,24},{5,25},{6,26},{7,27},{8,4},{9,5},{1... | collective-permute-start | bytes 1572872 | tf_op jit(solution)/shard_map/ppermute | solution.py:533
  472.8 35.9 %collective-permute-start.6 = (f32[128,1024]{1,0:T(8,128)S(1)}, f32[128,1024]{1,0:T(8,128)S(1)}, u32[]{:S(2)}, u32[]{:S(2)}) collective-permute-start(f32[128,1024]{1,0:T(8,128)S(1)} %get-tuple-element.36), channel_id=1, source_target_pairs={{0,8},{1,9},{2,10},{3,11},{4,16},{5,17},{6,18},{7,19},{8,12},{9,13... | collective-permute-start | bytes 1572872 | tf_op jit(solution)/shard_map/ppermute | solution.py:533
  491.9 16.9 %copy-start.9 = (f32[128,1024]{1,0:T(8,128)}, f32[128,1024]{1,0:T(8,128)S(1)}, u32[]{:S(2)}) copy-start(f32[128,1024]{1,0:T(8,128)S(1)} %collective-permute-done.5.refs_0_) | copy-start | bytes 1572868
  529.7 49.4 %collective-permute-start.7 = (f32[2,128,2048]{2,1,0:T(8,128)}, f32[2,128,2048]{2,1,0:T(8,128)S(1)}, u32[]{:S(2)}, u32[]{:S(2)}) collective-permute-start(f32[2,128,2048]{2,1,0:T(8,128)} %shard_map.121), channel_id=1, source_target_pairs={{0,0},{1,1},{2,2},{3,3},{16,4},{17,5},{18,6},{19,7},{4,8},{5,9},{6... | collective-permute-start | bytes 6291464 | tf_op jit(solution)/shard_map/ppermute | solution.py:565
  (6 other events, 6.3 us)

commit v4 on v3

--- a/solution.py
+++ b/solution.py
@@ -298,7 +298,7 @@
                 outs[branch][1, at, cols] = weight * sine
 
 
-def row_out(mat, work, out):
+def row_out(mat, work, out, spot=lambda k: k):
     outer, rows, double = work.shape
     inner = double // 2
 
@@ -307,8 +307,8 @@
         x = work[pl.ds(g * 2, 2)].reshape(2 * rows, double)
         y = product(halves(x), (mat[0], mat[1])).reshape(2, rows, double)
         for j in range(2):
-            out[g * 2 + j, 0] = y[j, :, :inner]
-            out[g * 2 + j, 1] = y[j, :, inner:]
+            out[spot(g * 2 + j), 0] = y[j, :, :inner]
+            out[spot(g * 2 + j), 1] = y[j, :, inner:]
 
 
 def twiddled(real, imag, tw, k):
@@ -320,36 +320,41 @@
     return real * c + imag * s, imag * c - real * s
 
 
-def first_kernel(field, mat, tw, out, work):
+def first_kernel(start, spot, field, mat, tw, out, work):
     outer, rows, double = work.shape
     inner = double // 2
 
     @pl.loop(0, rows // ROWS)
     def _(c):
-        at = pl.ds(pl.multiple_of(c * ROWS, ROWS), ROWS)
-        real = [field[0, at, a * inner : (a + 1) * inner] for a in range(outer)]
-        imag = [field[1, at, a * inner : (a + 1) * inner] for a in range(outer)]
+        base = pl.multiple_of(c * ROWS, ROWS)
+        at, source = pl.ds(base, ROWS), pl.ds(start + base, ROWS)
+        real = [field[0, source, a * inner : (a + 1) * inner] for a in range(outer)]
+        imag = [field[1, source, a * inner : (a + 1) * inner] for a in range(outer)]
         real, imag = small_fft(real, imag, -1)
         for k in range(outer):
             work[k, at, :inner], work[k, at, inner:] = twiddled(real[k], imag[k], tw, k)
 
-    row_out(mat, work, out)
-
-
-def column_forward_kernel(got, mat, tw, out, work):
-    outer, _, rows, lanes = got.shape
-
-    @pl.loop(0, rows // ROWS)
-    def _(c):
-        base = pl.multiple_of(c * ROWS, ROWS)
-        at = pl.ds(base, ROWS)
-        real = [got[a, 0, at, :] for a in range(outer)]
-        imag = [got[a, 1, at, :] for a in range(outer)]
-        real, imag = small_fft(real, imag, -1)
-        for k in range(outer):
-            cos, sin = tw[k, 0, at, :], tw[k, 1, at, :]
-            work[k, 0, at, :] = real[k] * cos - imag[k] * sin
-            work[k, 1, at, :] = real[k] * sin + imag[k] * cos
+    row_out(mat, work, out, spot)
+
+
+def column_forward_kernel(*refs):
+    pieces, (mat, tw, out, work) = refs[:-4], refs[-4:]
+    outer, _, rows, lanes = out.shape
+    part = rows // len(pieces)
+
+    for index, got in enumerate(pieces):
+
+        @pl.loop(0, part // ROWS)
+        def _(c):
+            base = pl.multiple_of(c * ROWS, ROWS)
+            source, at = pl.ds(base, ROWS), pl.ds(index * part + base, ROWS)
+            real = [got[a, 0, source, :] for a in range(outer)]
+            imag = [got[a, 1, source, :] for a in range(outer)]
+            real, imag = small_fft(real, imag, -1)
+            for k in range(outer):
+                cos, sin = tw[k, 0, at, :], tw[k, 1, at, :]
+                work[k, 0, at, :] = real[k] * cos - imag[k] * sin
+                work[k, 1, at, :] = real[k] * sin + imag[k] * cos
 
     @pl.loop(0, outer // 2)
     def _(g):
@@ -518,10 +523,22 @@
     along_y = number.astype(jnp.float32) / width_y
     fy2 = jnp.broadcast_to((along_y * along_y)[None, :], (ROWS, columns))
 
-    part_send = call(first_kernel, across, row_work, 4, wavefield[:, 0], row_fwd, row_tw)
-    sends = part_send.reshape(freq_count, freq_count, run, 2, rows, columns)
-    sends = sends.swapaxes(0, 1).reshape(across)
-    got = swap(swap(sends, "freq"), "slab")
+    def spot(k):
+        return (k // run) % freq_count * group + k // group * run + k % run
+
+    half = rows // 2
+    got = []
+    for piece in range(2):
+        sends = call(
+            functools.partial(first_kernel, piece * half, spot), (slabs, 2, half, columns),
+            (slabs, half, 2 * columns), 3, wavefield[:, 0], row_fwd, row_tw,
+        )
+        keep = lax.dynamic_slice_in_dim(sends, row * group, group, 0)
+        give = lax.dynamic_slice_in_dim(sends, (1 - row) * group, group, 0)
+        came = lax.ppermute(give, "freq", [(0, 1), (1, 0)])
+        pair = [jnp.where(row == y, keep, came) for y in range(freq_count)]
+        sends = jnp.concatenate(pair, axis=0)
+        got.append(swap(sends, "slab"))
 
     def grouped_velocity(values):
         moved = []
@@ -538,7 +555,7 @@
     for level in range(depth):
         last = level == depth - 1
         if level:
-            got = exchange(part_send)
+            got = [exchange(part_send)]
         else:
             got, velocity = lax.optimization_barrier((got, velocity))
         tiles = grouped_velocity(velocity[level])
@@ -547,7 +564,7 @@
             functools.partial(spread_kernel, slabs, width_x), across, None, 8, scal, fy2, scalars=1, outputs=2
         )
         weight = call(weight_kernel, (2, rows, width_y), None, 8, scal, order, *tiles, scalars=2, outputs=2)
-        spec = call(column_forward_kernel, across, across, 7, got, col_fwd, col_tw)
+        spec = call(column_forward_kernel, across, across, 7, *got, col_fwd, col_tw)
         back = []
         for branch in range(2):
             sent = call(column_back_kernel, across, across, 7, spec, shift[branch], col_inv, col_tw)

time: 586 us -> 580 us (0.990)
  blocking collectives: 27.6 us -> 0 us
  starting transfers between devices: 101 us -> 110 us
    all_to_all x1 -> x0, blocking collectives: 27.6 us -> none  [swap(): return lax.all_to_all(x, name, split_axis=0, concat_axis=0, tiled=True)]
    ppermute x0 -> x2, waiting for transfers between devices: none -> 23.4 us  [shards(): came = lax.ppermute(give, 'freq', [(0, 1), (1, 0)])]
    all_to_all x1 -> x2, waiting for transfers between devices: 36.2 us -> 17.2 us  [swap(): return lax.all_to_all(x, name, split_axis=0, concat_axis=0, tiled=True)]
    all_to_all x1 -> x2, starting transfers between devices: 7.51 us -> 12.2 us  [swap(): return lax.all_to_all(x, name, split_axis=0, concat_axis=0, tiled=True)]
    pallas_call x22 -> x23, Pallas kernels: 158 us -> 162 us  [call(): pl.pallas_call(body, out_shape=result if outputs == 1 else (result,) * ou...]
  transfers between devices with their start and end apart: 17 -> 20, of which waited for: 13 -> 16; matrix products, arithmetic and copies ran while one was open for 1% -> 2% of each run, Pallas kernels for 14% -> 15%
where the time goes in v4:
time: 580 us; the launch traced here: 574 us
  waiting for transfers between devices  278 us (48%)
  Pallas kernels  162 us (28%)
  starting transfers between devices  110 us (19%)
  local copies, waits for them, and re-layouts  15.8 us (3%)
  other arithmetic  8.34 us (1%)
    pallas_call x23, Pallas kernels, call(): pl.pallas_call(body, out_shape=result if outputs == 1 else (result,) * ou...  162 us
    ppermute x6, waiting for transfers between devices, grouped_velocity(): moved.append(lax.ppermute(values, both, route))  97.4 us
    all_to_all x8, waiting for transfers between devices, exchange(): lax.all_to_all(x, both, split_axis=0, concat_axis=0, tiled=True, axis_ind...  95.5 us
    all_to_all x8, starting transfers between devices, exchange(): lax.all_to_all(x, both, split_axis=0, concat_axis=0, tiled=True, axis_ind...  70.6 us
    ppermute x1, waiting for transfers between devices, shards(): return lax.ppermute(part_send, both, leave)[:, None]  44.3 us
    ppermute x2, waiting for transfers between devices, shards(): came = lax.ppermute(give, 'freq', [(0, 1), (1, 0)])  23.4 us
    ppermute x6, starting transfers between devices, grouped_velocity(): moved.append(lax.ppermute(values, both, route))  17.8 us
    all_to_all x2, waiting for transfers between devices, swap(): return lax.all_to_all(x, name, split_axis=0, concat_axis=0, tiled=True)  17.2 us
  transfers between devices with their start and end apart: 20, of which 16 were waited for; matrix products, arithmetic and copies ran while one was open for 2% of the time, Pallas kernels for 15%

profile of v4, /device:TPU:11, one launch (start us, length us, event | category | flops | bytes accessed | tf_op | source)
XLA Modules:
  0.0 573.7 jit_solution(15865490730282796085)
XLA Ops:
  7.2 11.6 %collective-permute-done = f32[8,2,64,128]{3,2,1,0:T(8,128)S(1)} collective-permute-done((f32[8,2,64,128]{3,2,1,0:T(8,128)S(1)}, f32[8,2,64,128]{3,2,1,0:T(8,128)S(1)}, u32[]{:S(2)}, u32[]{:S(2)}) %collective-permute-start) | collective-permute-done | bytes 524320 | tf_op jit(solution)/shard_map/ppermute | solution.py:538
  20.9 7.4 %all-to-all-start = ((f32[16,2,64,128]{3,2,1,0:T(8,128)}), f32[16,2,64,128]{3,2,1,0:T(8,128)S(1)}, u32[]{:S(2)}, u32[]{:S(2)}) async-start(f32[16,2,64,128]{3,2,1,0:T(8,128)} %pad_maximum_fusion), calls=%async_computation | async-start | bytes 2097152 | tf_op jit(solution)/shard_map/all_to_all | solution.py:513
  35.5 11.8 %collective-permute-done.1 = f32[8,2,64,128]{3,2,1,0:T(8,128)S(1)} collective-permute-done((f32[8,2,64,128]{3,2,1,0:T(8,128)S(1)}, f32[8,2,64,128]{3,2,1,0:T(8,128)S(1)}, u32[]{:S(2)}, u32[]{:S(2)}) %collective-permute-start.1) | collective-permute-done | bytes 524320 | tf_op jit(solution)/shard_map/ppermute | solution.py:538
  69.2 13.6 %all-to-all-done.1.refs_1_ = f32[16,2,64,128]{3,2,1,0:T(8,128)S(1)} async-done(((f32[16,2,64,128]{3,2,1,0:T(8,128)}), f32[16,2,64,128]{3,2,1,0:T(8,128)S(1)}, u32[]{:S(2)}, u32[]{:S(2)}) %all-to-all-start.1) | async-done | bytes 1048608 | tf_op jit(solution)/shard_map/all_to_all | solution.py:513
  90.5 7.4 %shard_map.106 = f32[16,2,128,128]{3,2,1,0:T(8,128)} custom-call(f32[16,2,128,128]{3,2,1,0:T(8,128)} %shard_map.102.spec, f32[16,2,128,128]{3,2,1,0:T(8,128)} %get-tuple-element.25.shift, bf16[2,256,256]{2,1,0:T(8,128)(2,1)} %constant.68.clone.mat.mat_next, f32[16,2,128,128]{3,2,1,0:T(8,128)} %constant.71.clone.refs_3_.tw.refs_2_), custom_call_target="tpu_custom_call" | custom-call | flops 2800000000 | bytes 21000000 | tf_op jit(solution)/shard_map/pallas_call | solution.py:465
  97.9 14.5 %all-to-all-start.3 = ((f32[16,2,128,128]{3,2,1,0:T(8,128)}), f32[16,2,128,128]{3,2,1,0:T(8,128)S(1)}, u32[]{:S(2)}, u32[]{:S(2)}) async-start(f32[16,2,128,128]{3,2,1,0:T(8,128)} %shard_map.106), calls=%async_computation.3 | async-start | bytes 4194304 | tf_op jit(solution)/shard_map/all_to_all | solution.py:516
  119.8 19.6 %all-to-all-done.3.got = f32[16,2,128,128]{3,2,1,0:T(8,128)S(1)} async-done(((f32[16,2,128,128]{3,2,1,0:T(8,128)}), f32[16,2,128,128]{3,2,1,0:T(8,128)S(1)}, u32[]{:S(2)}, u32[]{:S(2)}) %all-to-all-start.3) | async-done | bytes 2097184 | tf_op jit(solution)/shard_map/all_to_all | solution.py:516
  155.5 16.2 %collective-permute-done.3.refs_0_ = f32[128,1024]{1,0:T(8,128)S(1)} collective-permute-done((f32[128,1024]{1,0:T(8,128)S(1)}, f32[128,1024]{1,0:T(8,128)S(1)}, u32[]{:S(2)}, u32[]{:S(2)}) %collective-permute-start.3) | collective-permute-done | bytes 524320 | tf_op jit(solution)/shard_map/ppermute | solution.py:550
  171.7 15.2 %collective-permute-done.4.refs_1_ = f32[128,1024]{1,0:T(8,128)S(1)} collective-permute-done((f32[128,1024]{1,0:T(8,128)S(1)}, f32[128,1024]{1,0:T(8,128)S(1)}, u32[]{:S(2)}, u32[]{:S(2)}) %collective-permute-start.4) | collective-permute-done | bytes 524320 | tf_op jit(solution)/shard_map/ppermute | solution.py:550
  200.6 10.0 %shard_map.108 = f32[16,2,128,128]{3,2,1,0:T(8,128)} custom-call(f32[16,2,128,128]{3,2,1,0:T(8,128)} %all-to-all-done.2.got, f32[2,128,2048]{2,1,0:T(8,128)} %get-tuple-element.24.weight, f32[2,128,2048]{2,1,0:T(8,128)} %shard_map.107.part, bf16[2,256,256]{2,1,0:T(8,128)(2,1)} %constant.70.clone.refs_2_.mat.refs_1_, f32[16,2,8,128]{3,2,1,0:T(8,128)} %constant.69.clone.tw, ...), custom_call_target="tpu_custom_call" | custom-call | flops 3600000000 | bytes 27000000 | tf_op jit(solution)/shard_map/pallas_call | solution.py:465
  210.6 11.3 %all-to-all-start.4 = ((f32[16,2,128,128]{3,2,1,0:T(8,128)}), f32[16,2,128,128]{3,2,1,0:T(8,128)S(1)}, u32[]{:S(2)}, u32[]{:S(2)}) async-start(f32[16,2,128,128]{3,2,1,0:T(8,128)} %shard_map.108), calls=%async_computation.4 | async-start | bytes 4194304 | tf_op jit(solution)/shard_map/all_to_all | solution.py:516
  230.6 18.3 %all-to-all-done.4.refs_0_ = f32[16,2,128,128]{3,2,1,0:T(8,128)S(1)} async-done(((f32[16,2,128,128]{3,2,1,0:T(8,128)}), f32[16,2,128,128]{3,2,1,0:T(8,128)S(1)}, u32[]{:S(2)}, u32[]{:S(2)}) %all-to-all-start.4) | async-done | bytes 2097184 | tf_op jit(solution)/shard_map/all_to_all | solution.py:516
  256.9 7.4 %shard_map.113 = f32[16,2,128,128]{3,2,1,0:T(8,128)} custom-call(f32[16,2,128,128]{3,2,1,0:T(8,128)} %shard_map.109.spec, f32[16,2,128,128]{3,2,1,0:T(8,128)} %get-tuple-element.29.shift, bf16[2,256,256]{2,1,0:T(8,128)(2,1)} %constant.68.clone.mat.mat_next, f32[16,2,128,128]{3,2,1,0:T(8,128)} %constant.71.clone.refs_3_.tw.refs_2_), custom_call_target="tpu_custom_call" | custom-call | flops 2800000000 | bytes 21000000 | tf_op jit(solution)/shard_map/pallas_call | solution.py:465
  278.7 19.6 %all-to-all-done.6.got = f32[16,2,128,128]{3,2,1,0:T(8,128)S(1)} async-done(((f32[16,2,128,128]{3,2,1,0:T(8,128)}), f32[16,2,128,128]{3,2,1,0:T(8,128)S(1)}, u32[]{:S(2)}, u32[]{:S(2)}) %all-to-all-start.6) | async-done | bytes 2097184 | tf_op jit(solution)/shard_map/all_to_all | solution.py:516
  311.7 16.5 %collective-permute-done.5.refs_0_ = f32[128,1024]{1,0:T(8,128)S(1)} collective-permute-done((f32[128,1024]{1,0:T(8,128)S(1)}, f32[128,1024]{1,0:T(8,128)S(1)}, u32[]{:S(2)}, u32[]{:S(2)}) %collective-permute-start.5) | collective-permute-done | bytes 524320 | tf_op jit(solution)/shard_map/ppermute | solution.py:550
  328.2 16.7 %collective-permute-done.6.refs_1_ = f32[128,1024]{1,0:T(8,128)S(1)} collective-permute-done((f32[128,1024]{1,0:T(8,128)S(1)}, f32[128,1024]{1,0:T(8,128)S(1)}, u32[]{:S(2)}, u32[]{:S(2)}) %collective-permute-start.6) | collective-permute-done | bytes 524320 | tf_op jit(solution)/shard_map/ppermute | solution.py:550
  358.6 10.0 %shard_map.115 = f32[16,2,128,128]{3,2,1,0:T(8,128)} custom-call(f32[16,2,128,128]{3,2,1,0:T(8,128)} %all-to-all-done.5.got, f32[2,128,2048]{2,1,0:T(8,128)} %get-tuple-element.28.weight, f32[2,128,2048]{2,1,0:T(8,128)} %shard_map.114.part, bf16[2,256,256]{2,1,0:T(8,128)(2,1)} %constant.70.clone.refs_2_.mat.refs_1_, f32[16,2,8,128]{3,2,1,0:T(8,128)} %constant.69.clone.tw, ...), custom_call_target="tpu_custom_call" | custom-call | flops 3600000000 | bytes 27000000 | tf_op jit(solution)/shard_map/pallas_call | solution.py:465
  368.6 9.6 %all-to-all-start.7 = ((f32[16,2,128,128]{3,2,1,0:T(8,128)}), f32[16,2,128,128]{3,2,1,0:T(8,128)S(1)}, u32[]{:S(2)}, u32[]{:S(2)}) async-start(f32[16,2,128,128]{3,2,1,0:T(8,128)} %shard_map.115), calls=%async_computation.7 | async-start | bytes 4194304 | tf_op jit(solution)/shard_map/all_to_all | solution.py:516
  386.7 18.4 %all-to-all-done.7.refs_0_ = f32[16,2,128,128]{3,2,1,0:T(8,128)S(1)} async-done(((f32[16,2,128,128]{3,2,1,0:T(8,128)}), f32[16,2,128,128]{3,2,1,0:T(8,128)S(1)}, u32[]{:S(2)}, u32[]{:S(2)}) %all-to-all-start.7) | async-done | bytes 2097184 | tf_op jit(solution)/shard_map/all_to_all | solution.py:516
  413.2 7.4 %shard_map.120 = f32[16,2,128,128]{3,2,1,0:T(8,128)} custom-call(f32[16,2,128,128]{3,2,1,0:T(8,128)} %shard_map.116.spec, f32[16,2,128,128]{3,2,1,0:T(8,128)} %get-tuple-element.33.shift, bf16[2,256,256]{2,1,0:T(8,128)(2,1)} %constant.68.clone.mat.mat_next, f32[16,2,128,128]{3,2,1,0:T(8,128)} %constant.71.clone.refs_3_.tw.refs_2_), custom_call_target="tpu_custom_call" | custom-call | flops 2800000000 | bytes 21000000 | tf_op jit(solution)/shard_map/pallas_call | solution.py:465
  435.0 19.6 %all-to-all-done.9.got = f32[16,2,128,128]{3,2,1,0:T(8,128)S(1)} async-done(((f32[16,2,128,128]{3,2,1,0:T(8,128)}), f32[16,2,128,128]{3,2,1,0:T(8,128)S(1)}, u32[]{:S(2)}, u32[]{:S(2)}) %all-to-all-start.9) | async-done | bytes 2097184 | tf_op jit(solution)/shard_map/all_to_all | solution.py:516
  469.5 16.0 %collective-permute-done.7.refs_0_ = f32[128,1024]{1,0:T(8,128)S(1)} collective-permute-done((f32[128,1024]{1,0:T(8,128)S(1)}, f32[128,1024]{1,0:T(8,128)S(1)}, u32[]{:S(2)}, u32[]{:S(2)}) %collective-permute-start.7) | collective-permute-done | bytes 524320 | tf_op jit(solution)/shard_map/ppermute | solution.py:550
  485.5 16.8 %collective-permute-done.8.refs_1_ = f32[128,1024]{1,0:T(8,128)S(1)} collective-permute-done((f32[128,1024]{1,0:T(8,128)S(1)}, f32[128,1024]{1,0:T(8,128)S(1)}, u32[]{:S(2)}, u32[]{:S(2)}) %collective-permute-start.8) | collective-permute-done | bytes 524320 | tf_op jit(solution)/shard_map/ppermute | solution.py:550
  528.1 44.3 %collective-permute-done.9 = f32[2,128,2048]{2,1,0:T(8,128)S(1)} collective-permute-done((f32[2,128,2048]{2,1,0:T(8,128)}, f32[2,128,2048]{2,1,0:T(8,128)S(1)}, u32[]{:S(2)}, u32[]{:S(2)}) %collective-permute-start.9) | collective-permute-done | bytes 2097184 | tf_op jit(solution)/shard_map/ppermute | solution.py:582
  (81 shorter events, 214.3 us)
Async XLA Ops:
  5.9 12.9 %collective-permute-start = (f32[8,2,64,128]{3,2,1,0:T(8,128)S(1)}, f32[8,2,64,128]{3,2,1,0:T(8,128)S(1)}, u32[]{:S(2)}, u32[]{:S(2)}) collective-permute-start(f32[8,2,64,128]{3,2,1,0:T(8,128)S(1)} %constant_dynamic-slice_fusion.1), channel_id=1, source_target_pairs={{0,16},{16,0},{1,17},{17,1},{2,18},{18,2},{3,19},{19,3},{4,20},{20... | collective-permute-start | bytes 1572872 | tf_op jit(solution)/shard_map/ppermute | solution.py:538
  20.9 32.2 %all-to-all-start = ((f32[16,2,64,128]{3,2,1,0:T(8,128)}), f32[16,2,64,128]{3,2,1,0:T(8,128)S(1)}, u32[]{:S(2)}, u32[]{:S(2)}) async-start(f32[16,2,64,128]{3,2,1,0:T(8,128)} %pad_maximum_fusion), calls=%async_computation | async-start | bytes 2097152 | tf_op jit(solution)/shard_map/all_to_all | solution.py:513
  34.2 13.2 %collective-permute-start.1 = (f32[8,2,64,128]{3,2,1,0:T(8,128)S(1)}, f32[8,2,64,128]{3,2,1,0:T(8,128)S(1)}, u32[]{:S(2)}, u32[]{:S(2)}) collective-permute-start(f32[8,2,64,128]{3,2,1,0:T(8,128)S(1)} %constant_dynamic-slice_fusion), channel_id=1, source_target_pairs={{0,16},{16,0},{1,17},{17,1},{2,18},{18,2},{3,19},{19,3},{4,20},{20... | collective-permute-start | bytes 1572872 | tf_op jit(solution)/shard_map/ppermute | solution.py:538
  53.1 16.1 %copy-start.5 = (f32[16,2,64,128]{3,2,1,0:T(8,128)}, f32[16,2,64,128]{3,2,1,0:T(8,128)S(1)}, u32[]{:S(2)}) copy-start(f32[16,2,64,128]{3,2,1,0:T(8,128)S(1)} %all-to-all-done.refs_0_) | copy-start | bytes 3145732
  53.1 29.7 %all-to-all-start.1 = ((f32[16,2,64,128]{3,2,1,0:T(8,128)}), f32[16,2,64,128]{3,2,1,0:T(8,128)S(1)}, u32[]{:S(2)}, u32[]{:S(2)}) async-start(f32[16,2,64,128]{3,2,1,0:T(8,128)} %pad_maximum_fusion.1), calls=%async_computation.1 | async-start | bytes 2097152 | tf_op jit(solution)/shard_map/all_to_all | solution.py:513
  58.0 2.1 collective-permute-start.2
  97.9 41.5 %all-to-all-start.3 = ((f32[16,2,128,128]{3,2,1,0:T(8,128)}), f32[16,2,128,128]{3,2,1,0:T(8,128)S(1)}, u32[]{:S(2)}, u32[]{:S(2)}) async-start(f32[16,2,128,128]{3,2,1,0:T(8,128)} %shard_map.106), calls=%async_computation.3 | async-start | bytes 4194304 | tf_op jit(solution)/shard_map/all_to_all | solution.py:516
  140.8 59.9 %all-to-all-start.2 = ((f32[16,2,128,128]{3,2,1,0:T(8,128)}), f32[16,2,128,128]{3,2,1,0:T(8,128)}, u32[]{:S(2)}, u32[]{:S(2)}) async-start(f32[16,2,128,128]{3,2,1,0:T(8,128)} %shard_map.104), calls=%async_computation.2 | async-start | bytes 4194304 | tf_op jit(solution)/shard_map/all_to_all | solution.py:516
  149.3 22.5 %collective-permute-start.3 = (f32[128,1024]{1,0:T(8,128)S(1)}, f32[128,1024]{1,0:T(8,128)S(1)}, u32[]{:S(2)}, u32[]{:S(2)}) collective-permute-start(f32[128,1024]{1,0:T(8,128)S(1)} %get-tuple-element.40), channel_id=1, source_target_pairs={{0,0},{1,1},{2,2},{3,3},{4,24},{5,25},{6,26},{7,27},{8,4},{9,5},{1... | collective-permute-start | bytes 1572872 | tf_op jit(solution)/shard_map/ppermute | solution.py:550
  152.4 34.6 %collective-permute-start.4 = (f32[128,1024]{1,0:T(8,128)S(1)}, f32[128,1024]{1,0:T(8,128)S(1)}, u32[]{:S(2)}, u32[]{:S(2)}) collective-permute-start(f32[128,1024]{1,0:T(8,128)S(1)} %get-tuple-element.40), channel_id=1, source_target_pairs={{0,8},{1,9},{2,10},{3,11},{4,16},{5,17},{6,18},{7,19},{8,12},{9,13... | collective-permute-start | bytes 1572872 | tf_op jit(solution)/shard_map/ppermute | solution.py:550
  171.7 15.2 %copy-start.8 = (f32[128,1024]{1,0:T(8,128)}, f32[128,1024]{1,0:T(8,128)S(1)}, u32[]{:S(2)}) copy-start(f32[128,1024]{1,0:T(8,128)S(1)} %collective-permute-done.3.refs_0_) | copy-start | bytes 1572868
  210.6 38.2 %all-to-all-start.4 = ((f32[16,2,128,128]{3,2,1,0:T(8,128)}), f32[16,2,128,128]{3,2,1,0:T(8,128)S(1)}, u32[]{:S(2)}, u32[]{:S(2)}) async-start(f32[16,2,128,128]{3,2,1,0:T(8,128)} %shard_map.108), calls=%async_computation.4 | async-start | bytes 4194304 | tf_op jit(solution)/shard_map/all_to_all | solution.py:516
  264.3 34.0 %all-to-all-start.6 = ((f32[16,2,128,128]{3,2,1,0:T(8,128)}), f32[16,2,128,128]{3,2,1,0:T(8,128)S(1)}, u32[]{:S(2)}, u32[]{:S(2)}) async-start(f32[16,2,128,128]{3,2,1,0:T(8,128)} %shard_map.113), calls=%async_computation.6 | async-start | bytes 4194304 | tf_op jit(solution)/shard_map/all_to_all | solution.py:516
  299.6 58.9 %all-to-all-start.5 = ((f32[16,2,128,128]{3,2,1,0:T(8,128)}), f32[16,2,128,128]{3,2,1,0:T(8,128)}, u32[]{:S(2)}, u32[]{:S(2)}) async-start(f32[16,2,128,128]{3,2,1,0:T(8,128)} %shard_map.111), calls=%async_computation.5 | async-start | bytes 4194304 | tf_op jit(solution)/shard_map/all_to_all | solution.py:516
  306.7 21.5 %collective-permute-start.5 = (f32[128,1024]{1,0:T(8,128)S(1)}, f32[128,1024]{1,0:T(8,128)S(1)}, u32[]{:S(2)}, u32[]{:S(2)}) collective-permute-start(f32[128,1024]{1,0:T(8,128)S(1)} %get-tuple-element.39), channel_id=1, source_target_pairs={{0,0},{1,1},{2,2},{3,3},{4,24},{5,25},{6,26},{7,27},{8,4},{9,5},{1... | collective-permute-start | bytes 1572872 | tf_op jit(solution)/shard_map/ppermute | solution.py:550
  308.6 36.3 %collective-permute-start.6 = (f32[128,1024]{1,0:T(8,128)S(1)}, f32[128,1024]{1,0:T(8,128)S(1)}, u32[]{:S(2)}, u32[]{:S(2)}) collective-permute-start(f32[128,1024]{1,0:T(8,128)S(1)} %get-tuple-element.39), channel_id=1, source_target_pairs={{0,8},{1,9},{2,10},{3,11},{4,16},{5,17},{6,18},{7,19},{8,12},{9,13... | collective-permute-start | bytes 1572872 | tf_op jit(solution)/shard_map/ppermute | solution.py:550
  328.2 16.7 %copy-start.11 = (f32[128,1024]{1,0:T(8,128)}, f32[128,1024]{1,0:T(8,128)S(1)}, u32[]{:S(2)}) copy-start(f32[128,1024]{1,0:T(8,128)S(1)} %collective-permute-done.5.refs_0_) | copy-start | bytes 1572868
  368.6 36.6 %all-to-all-start.7 = ((f32[16,2,128,128]{3,2,1,0:T(8,128)}), f32[16,2,128,128]{3,2,1,0:T(8,128)S(1)}, u32[]{:S(2)}, u32[]{:S(2)}) async-start(f32[16,2,128,128]{3,2,1,0:T(8,128)} %shard_map.115), calls=%async_computation.7 | async-start | bytes 4194304 | tf_op jit(solution)/shard_map/all_to_all | solution.py:516
  420.6 34.0 %all-to-all-start.9 = ((f32[16,2,128,128]{3,2,1,0:T(8,128)}), f32[16,2,128,128]{3,2,1,0:T(8,128)S(1)}, u32[]{:S(2)}, u32[]{:S(2)}) async-start(f32[16,2,128,128]{3,2,1,0:T(8,128)} %shard_map.120), calls=%async_computation.9 | async-start | bytes 4194304 | tf_op jit(solution)/shard_map/all_to_all | solution.py:516
  455.9 60.0 %all-to-all-start.8 = ((f32[16,2,128,128]{3,2,1,0:T(8,128)}), f32[16,2,128,128]{3,2,1,0:T(8,128)}, u32[]{:S(2)}, u32[]{:S(2)}) async-start(f32[16,2,128,128]{3,2,1,0:T(8,128)} %shard_map.118), calls=%async_computation.8 | async-start | bytes 4194304 | tf_op jit(solution)/shard_map/all_to_all | solution.py:516
  462.9 22.5 %collective-permute-start.7 = (f32[128,1024]{1,0:T(8,128)S(1)}, f32[128,1024]{1,0:T(8,128)S(1)}, u32[]{:S(2)}, u32[]{:S(2)}) collective-permute-start(f32[128,1024]{1,0:T(8,128)S(1)} %get-tuple-element.38), channel_id=1, source_target_pairs={{0,0},{1,1},{2,2},{3,3},{4,24},{5,25},{6,26},{7,27},{8,4},{9,5},{1... | collective-permute-start | bytes 1572872 | tf_op jit(solution)/shard_map/ppermute | solution.py:550
  466.4 35.9 %collective-permute-start.8 = (f32[128,1024]{1,0:T(8,128)S(1)}, f32[128,1024]{1,0:T(8,128)S(1)}, u32[]{:S(2)}, u32[]{:S(2)}) collective-permute-start(f32[128,1024]{1,0:T(8,128)S(1)} %get-tuple-element.38), channel_id=1, source_target_pairs={{0,8},{1,9},{2,10},{3,11},{4,16},{5,17},{6,18},{7,19},{8,12},{9,13... | collective-permute-start | bytes 1572872 | tf_op jit(solution)/shard_map/ppermute | solution.py:550
  485.5 16.8 %copy-start.10 = (f32[128,1024]{1,0:T(8,128)}, f32[128,1024]{1,0:T(8,128)S(1)}, u32[]{:S(2)}) copy-start(f32[128,1024]{1,0:T(8,128)S(1)} %collective-permute-done.7.refs_0_) | copy-start | bytes 1572868
  523.2 49.2 %collective-permute-start.9 = (f32[2,128,2048]{2,1,0:T(8,128)}, f32[2,128,2048]{2,1,0:T(8,128)S(1)}, u32[]{:S(2)}, u32[]{:S(2)}) collective-permute-start(f32[2,128,2048]{2,1,0:T(8,128)} %shard_map.122), channel_id=1, source_target_pairs={{0,0},{1,1},{2,2},{3,3},{16,4},{17,5},{18,6},{19,7},{4,8},{5,9},{6... | collective-permute-start | bytes 6291464 | tf_op jit(solution)/shard_map/ppermute | solution.py:582
  (10 other events, 21.5 us)
